TPU v7x, 512 devices: a whole 4x8x8 slice. The times are simulated.
512 devices in a mesh: kv: 4 (over x), wide: 128 (over y, z, core).
Axes of the slice: x: 4, y: 8, z: 8, core: 2. Of those that a mesh axis runs over, the one named last changes fastest.
Arguments:
- stream_in: bfloat16 [256, 4, 2560], P('wide', None, 'kv'), may hold values from -8 to 8
- queries: bfloat16 [256, 4, 2560], P('wide', None, 'kv'), may hold values from -2.5 to 2.5
- new_kv: bfloat16 [256, 4, 2, 512], P('wide', None, None, 'kv'), may hold values from -2.5 to 2.5
- cache_keys: bfloat16 [4, 2048, 128, 128], P('kv', 'wide'), may hold values from -2.5 to 2.5
- cache_values: bfloat16 [4, 2048, 128, 128], P('kv', 'wide'), may hold values from -2.5 to 2.5
- lengths: int32 [32], replicated, may hold values from 1 to 4096, as said below
- page_table: int32 [32, 32], replicated, may hold values from -1 to 2047, as said below
- parents: int32 [256, 3], replicated, may hold values from 0 to 7
- routes: int32 [256, 4, 6], P('wide'), may hold values from 0 to 63, all different within a row; in each aligned block of 8 rows (0 to 7, 8 to 15, ..., all dimensions but the last counted through in order) at most 2 rows name the same one
- norm_gain: float32 [2560], replicated, may hold values from 0.5 to 1.5
- router: bfloat16 [2560, 64], replicated, may hold values from -0.01965332 to 0.01965332
- gate_w: bfloat16 [128, 2560, 768], P('wide', None, 'kv'), may hold values from -0.125 to 0.125
- up_w: bfloat16 [128, 2560, 768], P('wide', None, 'kv'), may hold values from -0.125 to 0.125
- down_w: bfloat16 [128, 768, 2560], P('wide', 'kv'), may hold values from -0.15625 to 0.15625
Outputs:
- stream_out: bfloat16 [256, 4, 2560], P('wide', None, 'kv')
Inputs may be any that keep to these rules, and one draw needn't show every extreme that they name: `lengths`: one group has exactly 4096 positions. `page_table`: entry [g, b] is the slot (index of wide times 16 plus the local slot) holding positions b * 128 to b * 128 + 127 of group g when b * 128 < lengths[g], and -1 otherwise; no slot is named twice; every slot of some index of wide is named. `parents`: entry [t, j] is a beam of t's own group. `routes`: within the rows of one index of wide (2 beams times 4 steps) no expert is named by more than 2 rows.
All inputs are finite; a program needn't handle non-finite values.
Results may differ from a plain program's by a relative error of at most 0.012.
Values may be sent and summed in bfloat16 or wider, within the bound.
A program may use at most 64 MiB of HBM per device.

v0:
```python
import math

import jax
import jax.numpy as jnp
from jax import lax
from jax.sharding import PartitionSpec as P

D = 2560
HD = 128
E = 64
TOP = 6
BEAMS = 8
BLK = 128
MOST = 2


def chain_tokens(parents, token_count, steps):
    tokens = jnp.arange(token_count, dtype=jnp.int32)
    group_base = tokens // BEAMS * BEAMS
    chain_table = []
    for step_now in range(steps):
        columns = [tokens] * steps
        current = tokens
        for earlier in range(step_now, 0, -1):
            current = group_base + parents[current, earlier - 1]
            columns[earlier - 1] = current
        chain_table.append(jnp.stack(columns, axis=1))
    return jnp.stack(chain_table, axis=1)


def local(
    stream_in,
    queries,
    new_kv,
    cache_keys,
    cache_values,
    lengths,
    page_table,
    parents,
    routes,
    norm_gain,
    router,
    gate_w,
    up_w,
    down_w,
):
    wide_index = lax.axis_index("wide")
    wide_count = lax.axis_size("wide")
    step_tok = stream_in.shape[0]
    steps = stream_in.shape[1]
    kv_local = new_kv.shape[3] // HD
    q_local = queries.shape[2] // HD
    head_ratio = q_local // kv_local
    groups = lengths.shape[0]
    token_count = groups * BEAMS
    slots_local = cache_keys.shape[1]
    score_scale = 1.0 / math.sqrt(HD)
    all_queries, all_kv = (
        lax.all_gather(queries, "wide", axis=0, tiled=True),
        lax.all_gather(new_kv, "wide", axis=0, tiled=True),
    )
    slot_ids = wide_index * slots_local + jnp.arange(slots_local, dtype=jnp.int32)
    slot_hits = page_table[None, :, :] == slot_ids[:, None, None]
    group_ids = jnp.arange(groups, dtype=jnp.int32)
    block_starts = jnp.arange(page_table.shape[1], dtype=jnp.int32) * BLK
    owner_group = jnp.sum(jnp.where(slot_hits, group_ids[None, :, None], 0), axis=(1, 2))
    slot_live = jnp.any(slot_hits, axis=(1, 2))
    block_limit = jnp.sum(
        jnp.where(slot_hits, lengths[None, :, None] - block_starts[None, None, :], 0), axis=(1, 2)
    )
    key_ok = (jnp.arange(BLK, dtype=jnp.int32)[None, :] < block_limit[:, None]).astype(jnp.float32)
    grouped = all_queries.reshape(groups, BEAMS, steps, kv_local, head_ratio, HD)
    picked = grouped[owner_group]
    scores = jnp.einsum(
        "nbskrd,knpd->nbskrp", picked, cache_keys, preferred_element_type=jnp.float32
    )
    weights = jnp.exp(scores * score_scale) * key_ok[:, None, None, None, None, :]
    rounded = weights.astype(jnp.bfloat16)
    numerator = jnp.einsum(
        "nbskrp,knpd->nbskrd", rounded, cache_values, preferred_element_type=jnp.float32
    )
    denominator = jnp.sum(rounded.astype(jnp.float32), axis=-1)
    onehot = ((owner_group[None, :] == group_ids[:, None]) & slot_live[None, :]).astype(jnp.float32)
    part_num = jnp.einsum("gn,nbskrd->gbskrd", onehot, numerator, precision=lax.Precision.HIGHEST)
    part_den = jnp.einsum("gn,nbskr->gbskr", onehot, denominator, precision=lax.Precision.HIGHEST)
    part_num = part_num.reshape(token_count, steps, q_local * HD)
    part_den = part_den.reshape(token_count, steps, q_local)
    first_token = wide_index * step_tok
    full_num, full_den = lax.psum((part_num, part_den), "wide")
    mine_num = lax.dynamic_slice_in_dim(full_num, first_token, step_tok, 0)
    mine_den = lax.dynamic_slice_in_dim(full_den, first_token, step_tok, 0)
    chains = chain_tokens(parents, token_count, steps)
    my_chain = lax.dynamic_slice_in_dim(chains, first_token, step_tok, 0)
    group_first = first_token // BEAMS * BEAMS
    local_chain = my_chain - group_first
    group_kv = lax.dynamic_slice_in_dim(all_kv, group_first, BEAMS, 0)
    history = group_kv[local_chain, jnp.arange(steps, dtype=jnp.int32)[None, None, :]]
    tail_keys = history[:, :, :, 0].reshape(step_tok, steps, steps, kv_local, HD)
    tail_values = history[:, :, :, 1].reshape(step_tok, steps, steps, kv_local, HD)
    own_queries = queries.reshape(step_tok, steps, kv_local, head_ratio, HD)
    tail_scores = jnp.einsum(
        "iskrd,isjkd->iskrj", own_queries, tail_keys, preferred_element_type=jnp.float32
    )
    causal = (jnp.arange(steps)[None, :] <= jnp.arange(steps)[:, None]).astype(jnp.float32)
    tail_weights = (jnp.exp(tail_scores * score_scale) * causal[None, :, None, None, :]).astype(
        jnp.bfloat16
    )
    tail_num = jnp.einsum(
        "iskrj,isjkd->iskrd", tail_weights, tail_values, preferred_element_type=jnp.float32
    )
    tail_den = jnp.sum(tail_weights.astype(jnp.float32), axis=-1)
    numer_all = mine_num.reshape(step_tok, steps, kv_local, head_ratio, HD) + tail_num
    denom_all = mine_den.reshape(step_tok, steps, kv_local, head_ratio) + tail_den
    attended = (
        (numer_all / denom_all[..., None])
        .astype(jnp.bfloat16)
        .reshape(step_tok, steps, q_local * HD)
    )
    residual = (stream_in.astype(jnp.float32) + attended.astype(jnp.float32)).astype(jnp.bfloat16)
    row_count = step_tok * steps
    full_rows = lax.all_gather(residual, "kv", axis=2, tiled=True)
    token_rows = full_rows.reshape(row_count, D).astype(jnp.float32)
    mean_square = jnp.mean(token_rows * token_rows, axis=1, keepdims=True)
    normed = (token_rows * lax.rsqrt(mean_square + 1e-06) * norm_gain[None, :]).astype(jnp.bfloat16)
    logits = jnp.dot(normed, router, preferred_element_type=jnp.float32)
    routed = routes.reshape(row_count, TOP)
    expert_ids = jnp.arange(E, dtype=jnp.int32)
    chosen = jnp.sum(
        jnp.where(routed[:, :, None] == expert_ids[None, None, :], logits[:, None, :], 0.0), axis=2
    )
    raised = jnp.exp(chosen)
    gate_share = raised / jnp.sum(raised, axis=1, keepdims=True)
    flat_routes = routed.reshape(-1)
    expert_hot = (flat_routes[:, None] == expert_ids[None, :]).astype(jnp.int32)
    before = jnp.cumsum(expert_hot, axis=0) - expert_hot
    place_in = jnp.sum(before * expert_hot, axis=1)
    row_of = jnp.arange(row_count * TOP, dtype=jnp.int32) // TOP
    slot_match = (expert_hot[:, :, None] == 1) & (
        place_in[:, None, None] == jnp.arange(MOST, dtype=jnp.int32)[None, None, :]
    )
    source_row = jnp.sum(jnp.where(slot_match, row_of[:, None, None] + 1, 0), axis=0) - 1
    source_row = jnp.where(source_row < 0, row_count, source_row)
    half_rows = jnp.repeat(source_row, 2, axis=0)
    row_width = normed.shape[1]
    padded = jnp.concatenate([normed, jnp.zeros((1, row_width), jnp.bfloat16)], axis=0)
    halves_local = gate_w.shape[0]
    outgoing = padded[half_rows].reshape(wide_count, halves_local, MOST, row_width)
    arrived_rows = lax.all_to_all(outgoing, "wide", split_axis=0, concat_axis=0, tiled=True)
    gate_out = jnp.einsum(
        "slmd,ldf->slmf", arrived_rows, gate_w, preferred_element_type=jnp.float32
    )
    up_out = jnp.einsum("slmd,ldf->slmf", arrived_rows, up_w, preferred_element_type=jnp.float32)
    hidden = (jax.nn.silu(gate_out) * up_out).astype(jnp.bfloat16)
    partial_value = jnp.einsum("slmf,lfd->slmd", hidden, down_w, preferred_element_type=jnp.float32)
    returned = lax.all_to_all(
        partial_value.astype(jnp.bfloat16), "wide", split_axis=0, concat_axis=0, tiled=True
    ).astype(partial_value.dtype)
    out_width = returned.shape[-1]
    per_expert = returned.reshape(E, 2, MOST, out_width).sum(axis=1).reshape(E * MOST, out_width)
    per_route = per_expert[flat_routes * MOST + place_in] * gate_share.reshape(-1)[:, None]
    combined = (
        per_route.reshape(row_count, TOP, out_width).sum(axis=1).reshape(step_tok, steps, out_width)
    )
    moe_part = lax.psum_scatter(
        combined.astype(jnp.bfloat16), "kv", scatter_dimension=2, tiled=True
    ).astype(jnp.float32)
    return (residual.astype(jnp.float32) + moe_part).astype(jnp.bfloat16)


def solution(mesh):
    return jax.shard_map(
        local,
        mesh=mesh,
        in_specs=(
            P("wide", None, "kv"),
            P("wide", None, "kv"),
            P("wide", None, None, "kv"),
            P("kv", "wide", None, None),
            P("kv", "wide", None, None),
            P(),
            P(),
            P(),
            P("wide", None, None),
            P(),
            P(),
            P("wide", None, "kv"),
            P("wide", None, "kv"),
            P("wide", "kv", None),
        ),
        out_specs=P("wide", None, "kv"),
        check_vma=False,
    )
```

profile of v0, /device:TPU:1, one launch (start us, length us, event | category | flops | bytes accessed | tf_op | source)
XLA Modules:
  0.0 760.1 jit_solution(7040916446946888398)
XLA Ops:
  6.5 0.7 all-gather.2.cloned.1.call-update
  7.3 0.7 reshape.499
  8.0 0.7 copy.64
  8.7 58.9 %all_gather.10 = bf16[256,4,2,128]{3,1,2,0:T(4,128)(2,1)S(1)} all-gather(bf16[2,4,2,128]{3,1,2,0:T(4,128)(2,1)S(1)} %copy.64), channel_id=1, replica_groups=mesh['kv'=4,'wide'=128] {'wide'}, dimensions={0}, use_global_device_ids=true | all-gather | bytes 528384 | tf_op jit(solution)/shard_map/all_gather | solution.py:60
  67.7 2.8 gather_fusion.2
  70.5 2.5 gather_fusion.4
  73.0 2.5 gather_fusion.5
  75.5 2.5 gather_fusion.6
  78.0 2.5 gather_fusion.3
  80.5 2.5 gather_fusion.1
  83.4 0.7 gather_fusion.7
  84.4 0.7 fusion.46
  85.5 0.5 compare_reduce_fusion
  86.0 12.7 %all-gather.2.cloned.1.call-done = bf16[256,4,640]{2,1,0:T(4,128)(2,1)} async-done(((bf16[2,4,640]{2,1,0:T(4,128)(2,1)}), bf16[256,4,640]{2,1,0:T(4,128)(2,1)}) %all-gather.2.cloned.1.call-update) | async-done | bytes 1310736 | tf_op jit(solution)/shard_map/all_gather | solution.py:59
  98.7 2.8 reshape.600
  101.5 2.2 copy.60
  103.7 2.0 gather_fusion
  105.8 0.6 convert_reduce_fusion.1
  106.4 0.4 copy-done.4
  106.8 0.3 fusion.37
  107.1 1.9 fusion.9
  109.1 3.5 copy.62
  112.6 4.7 reshape.496
  117.8 0.4 fusion.52
  118.3 0.8 copy.87
  119.1 488.7 %psum.15 = f32[256,4,5]{2,1,0:T(4,128)S(1)} all-reduce(f32[256,4,5]{2,1,0:T(4,128)S(1)} %bitcast.164), channel_id=1, replica_groups=mesh['kv'=4,'wide'=128] {'wide'}, use_global_device_ids=true, to_apply=%region_5.6 | all-reduce | flops 5120 | bytes 40960 | tf_op jit(solution)/shard_map/psum | solution.py:89
  607.9 0.9 constant_dynamic-slice_fusion.1
  608.8 0.2 fusion.30
  609.0 9.1 %all_gather.11 = bf16[2,4,2560]{2,1,0:T(4,128)(2,1)S(1)} all-gather(bf16[2,4,640]{2,1,0:T(4,128)(2,1)S(1)} %add_convert_fusion.1), channel_id=1, replica_groups=mesh['kv'=4,'wide'=128] {'kv'}, dimensions={2}, use_global_device_ids=true | all-gather | bytes 51200 | tf_op jit(solution)/shard_map/all_gather | solution.py:121
  618.5 1.4 gather_fusion.8
  619.9 1.4 reshape.503
  621.3 51.2 %all_to_all.10 = bf16[128,1,2,2560]{3,2,1,0:T(2,128)(2,1)S(1)} all-to-all(bf16[128,1,2,2560]{3,2,1,0:T(2,128)(2,1)} %bitcast.162), channel_id=1, replica_groups=mesh['kv'=4,'wide'=128] {'wide'}, dimensions={0} | all-to-all | bytes 2621440 | tf_op jit(solution)/shard_map/all_to_all | solution.py:148
  672.5 0.6 fusion.13
  673.1 0.6 copy-done.3
  673.7 2.8 fusion
  676.4 3.7 copy.74
  680.2 7.7 %all-to-all-start.1 = ((bf16[128,1,2,2560]{3,2,1,0:T(2,128)(2,1)}), bf16[128,1,2,2560]{3,2,1,0:T(2,128)(2,1)S(1)}, u32[]{:S(2)}, u32[]{:S(2)}) async-start(bf16[128,1,2,2560]{3,2,1,0:T(2,128)(2,1)} %copy.74), calls=%async_computation.1 | async-start | bytes 2621440 | tf_op jit(solution)/shard_map/all_to_all | solution.py:155
  688.6 34.8 %all-to-all-done.1 = bf16[128,1,2,2560]{3,2,1,0:T(2,128)(2,1)S(1)} async-done(((bf16[128,1,2,2560]{3,2,1,0:T(2,128)(2,1)}), bf16[128,1,2,2560]{3,2,1,0:T(2,128)(2,1)S(1)}, u32[]{:S(2)}, u32[]{:S(2)}) %all-to-all-start.1) | async-done | bytes 1310752 | tf_op jit(solution)/shard_map/all_to_all | solution.py:155
  723.5 2.7 convert_reduce_fusion
  726.2 2.2 reshape.511
  728.3 0.7 gather_fusion.9
  729.2 0.3 multiply_reduce_fusion
  729.5 1.0 copy.88
  730.5 1.5 reshape.601
  732.0 19.7 %reduce-scatter.4.cloned.1.call-done = bf16[640,8]{1,0:T(8,128)(2,1)} async-done(((bf16[2560,8]{1,0:T(8,128)(2,1)}), bf16[640,8]{1,0:T(8,128)(2,1)}) %reduce-scatter.4.cloned.1.call-update) | async-done | bytes 10256
  751.7 1.1 reshape.602
  752.8 0.2 copy.89
  753.0 0.6 add_convert_fusion
  (89 shorter events, 2.8 us)
Async XLA Ops:
  6.5 666.5 %copy-start = (bf16[1,192,2560]{2,1,0:T(8,128)(2,1)S(1)}, bf16[1,192,2560]{2,1,0:T(8,128)(2,1)}, u32[]{:S(2)}) copy-start(bf16[1,192,2560]{2,1,0:T(8,128)(2,1)} %param.27) | copy-start | bytes 2949124
  6.5 63.9 %copy-start.2 = (s32[256]{0:T(256)S(1)}, s32[256]{0:T(256)}, u32[]{:S(2)}) copy-start(s32[256]{0:T(256)} %constant.251) | copy-start | bytes 3076
  6.5 61.1 %copy-start.1 = (s32[256,3]{0,1:T(4,128)S(1)}, s32[256,3]{0,1:T(4,128)}, u32[]{:S(2)}) copy-start(s32[256,3]{0,1:T(4,128)} %param.21) | copy-start | bytes 9220
  6.5 92.2 %all-gather.2.cloned.1.call-start = ((), (), s32[]{:S(2)}) async-start(), calls=%async_computation.3 | async-start | bytes 1320960 | tf_op jit(solution)/shard_map/all_gather | solution.py:59
  7.3 600.6 %all-reduce.6.cloned.1.call-start = ((), (), s32[]{:S(2)}) async-start(), calls=%async_computation.4 | async-start | bytes 5242880 | tf_op jit(solution)/shard_map/psum | solution.py:89
  77.9 6.1 copy-start.7
  78.0 6.3 copy-start.10
  78.0 6.4 copy-start.6
  103.7 2.1 copy-start.12
  105.8 1.0 copy-start.4
  117.8 491.2 %copy-start.9 = (bf16[2,4,640]{2,1,0:T(4,128)(2,1)S(1)}, bf16[2,4,640]{2,1,0:T(4,128)(2,1)}, u32[]{:S(2)}) copy-start(bf16[2,4,640]{2,1,0:T(4,128)(2,1)} %param.14) | copy-start | bytes 30724
  118.3 500.1 %copy-start.8 = (f32[2560]{0:T(1024)S(1)}, f32[2560]{0:T(1024)}, u32[]{:S(2)}) copy-start(f32[2560]{0:T(1024)} %param.23) | copy-start | bytes 30724
  621.3 51.2 %copy-start.11 = (bf16[1,2560,192]{1,2,0:T(8,128)(2,1)S(1)}, bf16[1,2560,192]{1,2,0:T(8,128)(2,1)}, u32[]{:S(2)}) copy-start(bf16[1,2560,192]{1,2,0:T(8,128)(2,1)} %param.25) | copy-start | bytes 2949124
  672.5 1.2 copy-start.3
  680.2 8.0 %copy-start.5 = (bf16[2560,64]{0,1:T(8,128)(2,1)S(1)}, bf16[2560,64]{0,1:T(8,128)(2,1)}, u32[]{:S(2)}) copy-start(bf16[2560,64]{0,1:T(8,128)(2,1)} %param.24) | copy-start | bytes 983044
  680.2 43.3 %all-to-all-start.1 = ((bf16[128,1,2,2560]{3,2,1,0:T(2,128)(2,1)}), bf16[128,1,2,2560]{3,2,1,0:T(2,128)(2,1)S(1)}, u32[]{:S(2)}, u32[]{:S(2)}) async-start(bf16[128,1,2,2560]{3,2,1,0:T(2,128)(2,1)} %copy.74), calls=%async_computation.1 | async-start | bytes 2621440 | tf_op jit(solution)/shard_map/all_to_all | solution.py:155
  687.9 63.8 %reduce-scatter.4.cloned.1.call-start = ((), (), s32[]{:S(2)}) async-start(), calls=%async_computation.5 | async-start | bytes 819200
Sparse Core Ops, SparseCore 0:
  10.6 88.1 all-gather.1
  117.5 197.3 all-reduce.5
  732.1 19.5 reduce-scatter.3
where the time goes:
time: 762 us; the launch traced here: 760 us
  blocking collectives  608 us (80%)
  waiting for transfers between devices  68 us (9%)
  local copies, waits for them, and re-layouts  49.6 us (7%)
  between operations  13.6 us (2%)
  starting transfers between devices  7.81 us (1%)
    psum x1, blocking collectives, local(): full_num, full_den = lax.psum((part_num, part_den), 'wide')  489 us
    all_gather x1, blocking collectives, local(): lax.all_gather(new_kv, 'wide', axis=0, tiled=True)  58.9 us
    all_to_all x1, blocking collectives, local(): lax.all_to_all(outgoing, 'wide', split_axis=0, concat_axis=0, tiled=True)  51.2 us
    all_to_all x1, waiting for transfers between devices, local(): lax.all_to_all(partial_value.astype(jnp.bfloat16), 'wide', split_axis=0,...  34.8 us
    unnamed x4, waiting for transfers between devices  20.4 us
  transfers between devices with their start and end apart: 4, of which 3 were waited for; matrix products, arithmetic and copies ran while one was open for 3% of the time, Pallas kernels for 0%

commit v1 on v0

v1 whole, which is shorter than its diff:
```python
import functools
import math

import jax
import jax.numpy as jnp
from jax import lax
from jax.experimental import pallas as pl
from jax.experimental.pallas import tpu as pltpu
from jax.sharding import PartitionSpec as P

MESH = pl.DeviceIdType.MESH
HD = 128
BEAMS = 8
BLK = 128
MOST = 2
F32 = jnp.float32
BF16 = jnp.bfloat16


def far_first(n):
    order = sorted(range(1, n), key=lambda d: -min(d, n - d))
    return order


def near_first(n):
    return sorted(range(1, n), key=lambda d: min(d, n - d))


def rcopy(src, dst, send_sem, recv_sem, device):
    return pltpu.make_async_remote_copy(
        src_ref=src,
        dst_ref=dst,
        send_sem=send_sem,
        recv_sem=recv_sem,
        device_id=device,
        device_id_type=MESH,
    )


def dot(x, y):
    return jnp.dot(x, y, preferred_element_type=F32)


def iota(shape, axis):
    return lax.broadcasted_iota(jnp.int32, shape, axis)


def kernel(
    n,
    kv_count,
    heads,
    stream_ref,
    query_ref,
    newkv_ref,
    keys_hbm,
    values_hbm,
    lengths_ref,
    table_ref,
    parents_ref,
    routes_ref,
    gain_ref,
    router_hbm,
    gate_hbm,
    up_hbm,
    down_hbm,
    out_ref,
    keys,
    values,
    router,
    gate,
    up,
    down,
    load_sem,
    qfull,
    kvgroup,
    q_sems,
    slot_group,
    slot_limit,
    slot_prev,
    group_last,
    sums,
    part,
    sibling_part,
    core_sum,
    b_parts,
    b_sum,
    a_parts,
    part_sems,
    resid,
    resid_all,
    x_sems,
    outgoing,
    mid_rows,
    mid_perm,
    rows,
    row_sems,
    expert_part,
    expert_sib,
    x_send,
    x_recv,
    back_a,
    back_mid,
    back_perm,
    back_rows,
    back_sems,
):
    kv = lax.axis_index("kv")
    w = lax.axis_index("wide")
    c = w % 2
    z = (w // 2) % n
    y = w // (2 * n)
    a = z + c * (y - z)
    b = y + c * (z - y)
    stride_a = 2 + c * (2 * n - 2)
    stride_b = 2 * n - c * (2 * n - 2)
    sib = {"wide": w + 1 - 2 * c}
    width = heads * HD
    row_count = query_ref.shape[0]
    slots = keys.shape[0]
    groups = lengths_ref.shape[0]
    blocks = table_ref.shape[1]
    steps = parents_ref.shape[1] + 1
    top = routes_ref.shape[1]
    scale = 1.0 / math.sqrt(HD)

    def dev_a(j):
        return {"wide": w + (j - a) * stride_a}

    def dev_b(j):
        return {"wide": w + (j - b) * stride_b}

    def dev_x(j):
        return {"kv": j}

    group_first = w // 4 * 4
    group_place = w % 4

    loads = [
        pltpu.make_async_copy(src, dst, load_sem.at[i])
        for i, (src, dst) in enumerate(
            [
                (keys_hbm.at[0], keys),
                (values_hbm.at[0], values),
                (router_hbm, router),
                (gate_hbm.at[0], gate),
                (up_hbm.at[0], up),
                (down_hbm.at[0], down),
            ]
        )
    ]
    own_query = pltpu.make_async_copy(query_ref, qfull.at[c, b, a], load_sem.at[6])
    own_kv = pltpu.make_async_copy(newkv_ref, kvgroup.at[group_place], load_sem.at[7])
    own_query.start()
    own_kv.start()
    for load in loads:
        load.start()

    barrier = pltpu.get_barrier_semaphore()
    greeted = 0
    for d in far_first(n):
        for device in (dev_a((a + d) % n), dev_b((b + d) % n)):
            pl.semaphore_signal(barrier, inc=1, device_id=device, device_id_type=MESH)
            greeted += 1
    for d in range(1, kv_count):
        pl.semaphore_signal(
            barrier, inc=1, device_id=dev_x((kv + d) % kv_count), device_id_type=MESH
        )
        greeted += 1
    for d in range(1, 4):
        pl.semaphore_signal(
            barrier,
            inc=1,
            device_id={"wide": group_first + (group_place + d) % 4},
            device_id_type=MESH,
        )
        greeted += 1
    pl.semaphore_wait(barrier, greeted)

    sent = []

    def send(copy):
        copy.start()
        sent.append(copy)

    q_send, q_recv = q_sems
    for d in far_first(n):
        send(
            rcopy(query_ref, qfull.at[c, b, a], q_send.at[0, d], q_recv.at[0, a], dev_a((a + d) % n))
        )
    for d in range(1, 4):
        peer = group_first + (group_place + d) % 4
        send(
            rcopy(
                newkv_ref,
                kvgroup.at[group_place],
                q_send.at[3, d],
                q_recv.at[3, group_place],
                {"wide": peer},
            )
        )

    table = table_ref[...]
    place = iota((groups, blocks), 0) * blocks + iota((groups, blocks), 1) + 1
    owners = []
    for s in range(slots):
        code = jnp.max(jnp.where(table == w * slots + s, place, 0))
        live = jnp.minimum(code, 1)
        spot = jnp.maximum(code - 1, 0)
        group = spot // blocks
        slot_group[s] = group
        slot_limit[s] = live * (lengths_ref[group] - spot % blocks * BLK)
        owners.append(jnp.where(code > 0, group, -1))
    for s in range(slots):
        before = jnp.int32(slots)
        for r in range(s):
            before = jnp.where(owners[r] == owners[s], r, before)
        slot_prev[s] = before
    for g in range(groups):
        last = jnp.int32(slots)
        for s in range(slots):
            last = jnp.where(owners[s] == g, s, last)
        group_last[g] = last
    sums[slots] = jnp.zeros(sums.shape[1:], F32)

    own_query.wait()
    for d in near_first(n):
        j = (a + d) % n
        rcopy(query_ref, qfull.at[c, b, j], q_send.at[0, d], q_recv.at[0, j], dev_a(j)).wait_recv()
    for d in far_first(n):
        send(
            rcopy(
                qfull.at[c, b],
                qfull.at[c, b],
                q_send.at[1, d],
                q_recv.at[1, b],
                dev_b((b + d) % n),
            )
        )
    send(rcopy(qfull.at[c, b], qfull.at[c, b], q_send.at[2, 0], q_recv.at[2, b], sib))
    for d in near_first(n):
        j = (b + d) % n
        rcopy(
            qfull.at[c, b], qfull.at[c, j], q_send.at[1, d], q_recv.at[1, j], dev_b(j)
        ).wait_recv()
        send(rcopy(qfull.at[c, j], qfull.at[c, j], q_send.at[2, d], q_recv.at[2, j], sib))
    for j in range(n):
        rcopy(
            qfull.at[1 - c, j], qfull.at[1 - c, j], q_send.at[2, j], q_recv.at[2, j], sib
        ).wait_recv()

    loads[0].wait()
    loads[1].wait()
    half_n = n // 2
    group_rows = 4 * row_count

    def one_slot(s, carry):
        group = slot_group[s]
        gy = group // half_n
        gz = group % half_n * 2
        q = jnp.concatenate(
            [qfull[0, gy, gz], qfull[0, gy, gz + 1], qfull[1, gz, gy], qfull[1, gz + 1, gy]],
            axis=0,
        )
        q = jnp.concatenate([q[:, r * HD : (r + 1) * HD] for r in range(heads)], axis=0)
        scores = lax.dot_general(
            q, keys[s], (((1,), (1,)), ((), ())), preferred_element_type=F32
        )
        ok = iota(scores.shape, 1) < slot_limit[s]
        weights = jnp.where(ok, jnp.exp(scores * scale), 0.0).astype(BF16)
        extended = jnp.concatenate([values[s], jnp.ones((BLK, HD), BF16)], axis=1)
        sums[s] = dot(weights, extended) + sums[slot_prev[s]]
        return carry

    lax.fori_loop(0, slots, one_slot, 0)

    lane = iota((row_count, HD), 1)

    def one_group(g, carry):
        last = group_last[g]
        gy = g // half_n
        gz = g % half_n * 2
        for core in range(2):
            for zl in range(2):
                at = (core, gy, gz + zl) if core == 0 else (core, gz + zl, gy)
                dens = jnp.zeros((row_count, HD), F32)
                for r in range(heads):
                    first = r * group_rows + (core * 2 + zl) * row_count
                    block = sums[last, pl.ds(first, row_count), :]
                    part[at + (slice(None), slice(r * HD, (r + 1) * HD))] = block[:, :HD].astype(
                        BF16
                    )
                    dens = jnp.where(lane % 8 == r, block[:, HD:], dens)
                high = dens.astype(BF16).astype(F32)
                part[at + (slice(None), slice(width, width + HD))] = jnp.where(
                    lane < 8, high, dens - high
                ).astype(BF16)
        return carry

    lax.fori_loop(0, groups, one_group, 0)

    p_send, p_recv = part_sems
    for d in far_first(n) + [0]:
        j = (a + d) % n
        send(rcopy(part.at[1 - c, j], sibling_part.at[j], p_send.at[0, d], p_recv.at[0, j], sib))
    for d in far_first(n) + [0]:
        j = (b + d) % n
        rcopy(
            part.at[1 - c, j], sibling_part.at[j], p_send.at[0, d], p_recv.at[0, j], sib
        ).wait_recv()
        core_sum[j] = (part[c, j].astype(F32) + sibling_part[j].astype(F32)).astype(BF16)
        if d:
            send(rcopy(core_sum.at[j], b_parts.at[b], p_send.at[1, d], p_recv.at[1, b], dev_b(j)))

    for j in range(1, 4):
        p = (group_place + j) % 4
        rcopy(
            newkv_ref, kvgroup.at[p], q_send.at[3, j], q_recv.at[3, p], {"wide": group_first + p}
        ).wait_recv()
    own_kv.wait()
    key_rows = 4 * row_count
    tail_kv = jnp.concatenate([kvgroup[i] for i in range(4)], axis=0)
    row_id = iota((row_count, key_rows), 0)
    key_id = iota((row_count, key_rows), 1)
    wanted = jnp.full((row_count, key_rows), -1, jnp.int32)
    token_base = w // 4 * BEAMS
    for i in range(row_count // steps):
        for s in range(steps):
            beam = group_place * (row_count // steps) + i
            for j in range(s, -1, -1):
                wanted = jnp.where(
                    (row_id == i * steps + s) & (key_id % steps == j), beam, wanted
                )
                if j:
                    beam = parents_ref[token_base + beam, j - 1]
    allowed = wanted == key_id // steps
    tail_q = jnp.concatenate([query_ref[:, r * HD : (r + 1) * HD] for r in range(heads)], axis=0)
    tail_scores = lax.dot_general(
        tail_q, tail_kv[:, :HD], (((1,), (1,)), ((), ())), preferred_element_type=F32
    )
    tail_ok = jnp.concatenate([allowed.astype(F32)] * heads, axis=0)
    tail_w = jnp.where(tail_ok > 0, jnp.exp(tail_scores * scale), 0.0).astype(BF16)
    tail_num = dot(tail_w, tail_kv[:, HD:])
    tail_den = jnp.sum(tail_w.astype(F32), axis=1, keepdims=True)

    cols = n * n * MOST
    col = iota((1, cols), 1)
    col_b = col // (n * MOST)
    col_a = col // MOST % n
    col_place = col % MOST
    col_expert = col_b * n + col_a + c * ((col_a - col_b) * (n - 1))
    count = jnp.zeros((1, cols), jnp.int32)
    hits = []
    picks = []
    for r in range(row_count):
        hit = jnp.zeros((1, cols), jnp.int32)
        for i in range(top):
            hit = jnp.where(col_expert == routes_ref[r, i], 1, hit)
        picks.append(jnp.where(count == col_place, hit, 0))
        hits.append(hit)
        count = count + hit
    hit_all = jnp.concatenate(hits, axis=0)
    pick_all = jnp.concatenate(picks, axis=0).astype(F32)

    for d in near_first(n):
        j = (b + d) % n
        rcopy(core_sum.at[j], b_parts.at[j], p_send.at[1, d], p_recv.at[1, j], dev_b(j)).wait_recv()
    for d in far_first(n) + [0]:
        j = (a + d) % n
        total = core_sum[b, j].astype(F32)
        for e in range(1, n):
            total = total + b_parts[(b + e) % n, j].astype(F32)
        b_sum[j] = total.astype(BF16)
        if d:
            send(rcopy(b_sum.at[j], a_parts.at[a], p_send.at[2, d], p_recv.at[2, a], dev_a(j)))
    total = b_sum[a].astype(F32)
    for d in near_first(n):
        j = (a + d) % n
        rcopy(b_sum.at[j], a_parts.at[j], p_send.at[2, d], p_recv.at[2, j], dev_a(j)).wait_recv()
        total = total + a_parts[j].astype(F32)

    attended = []
    for r in range(heads):
        num = total[:, r * HD : (r + 1) * HD] + tail_num[r * row_count : (r + 1) * row_count]
        den = (
            total[:, width + r : width + r + 1]
            + total[:, width + 8 + r : width + 9 + r]
            + tail_den[r * row_count : (r + 1) * row_count]
        )
        attended.append((num / den).astype(BF16).astype(F32))
    residual = (stream_ref[...].astype(F32) + jnp.concatenate(attended, axis=1)).astype(BF16)
    resid[...] = residual

    x_ssem, x_rsem = x_sems
    for d in range(1, kv_count):
        send(
            rcopy(
                resid, resid_all.at[kv], x_ssem.at[0, d], x_rsem.at[0, kv], dev_x((kv + d) % kv_count)
            )
        )
    resid_all[kv] = residual
    loads[2].wait()
    for d in range(1, kv_count):
        j = (kv + d) % kv_count
        rcopy(resid, resid_all.at[j], x_ssem.at[0, d], x_rsem.at[0, j], dev_x(j)).wait_recv()
    full = jnp.concatenate([resid_all[i].astype(F32) for i in range(kv_count)], axis=1)
    mean_square = jnp.sum(full * full, axis=1, keepdims=True) / full.shape[1]
    normed = (full * lax.rsqrt(mean_square + 1e-06) * gain_ref[...]).astype(BF16)

    r_send, r_recv = row_sems
    chosen_rows = lax.dot_general(
        pick_all.astype(BF16), normed, (((0,), (0,)), ((), ())), preferred_element_type=F32
    ).astype(BF16)
    block_rows = n * MOST
    outgoing[...] = chosen_rows.reshape(outgoing.shape)
    for d in far_first(n):
        j = (b + d) % n
        send(rcopy(outgoing.at[j], mid_rows.at[b], r_send.at[0, d], r_recv.at[0, b], dev_b(j)))
    mid_rows[b] = outgoing[b]

    logits = dot(normed, router[...])
    experts = logits.shape[1]
    spread = (iota((experts, cols), 0) == col_expert).astype(F32)
    col_logits = lax.dot_general(
        logits,
        spread,
        (((1,), (0,)), ((), ())),
        preferred_element_type=F32,
        precision=lax.Precision.HIGHEST,
    )
    raised = jnp.where(hit_all > 0, jnp.exp(jnp.where(hit_all > 0, col_logits, 0.0)), 0.0)
    total_raised = jnp.sum(jnp.where(col_place == 0, raised, 0.0), axis=1, keepdims=True)
    share = raised / total_raised * pick_all
    share_high = share.astype(BF16)
    share_low = (share - share_high.astype(F32)).astype(BF16)

    out_i = iota((cols, cols), 0)
    swapped = out_i // MOST % n * block_rows + out_i // block_rows * MOST + out_i % MOST
    swap = (iota((cols, cols), 1) == swapped).astype(BF16)

    for d in near_first(n):
        j = (b + d) % n
        rcopy(outgoing.at[j], mid_rows.at[j], r_send.at[0, d], r_recv.at[0, j], dev_b(j)).wait_recv()
    model = full.shape[1]
    mid = mid_rows[...].reshape(cols, model)
    mid_perm[...] = dot(swap, mid).astype(BF16).reshape(mid_perm.shape)
    for d in far_first(n):
        j = (a + d) % n
        send(rcopy(mid_perm.at[j], rows.at[c, a], r_send.at[1, d], r_recv.at[1, a], dev_a(j)))
    send(rcopy(mid_perm.at[a], rows.at[c, a], r_send.at[2, 0], r_recv.at[2, a], sib))
    rows[c, a] = mid_perm[a]
    for d in near_first(n):
        j = (a + d) % n
        rcopy(mid_perm.at[j], rows.at[c, j], r_send.at[1, d], r_recv.at[1, j], dev_a(j)).wait_recv()
        send(rcopy(rows.at[c, j], rows.at[c, j], r_send.at[2, d], r_recv.at[2, j], sib))
    for i in range(3, 6):
        loads[i].wait()

    def expert(core):
        x = rows[core].reshape(cols, model)
        gated = dot(x, gate[...])
        lifted = dot(x, up[...])
        hidden = (gated / (1.0 + jnp.exp(-gated)) * lifted).astype(BF16)
        return dot(hidden, down[...])

    own_out = expert(c)
    for j in range(n):
        rcopy(
            rows.at[1 - c, j], rows.at[1 - c, j], r_send.at[2, j], r_recv.at[2, j], sib
        ).wait_recv()
    expert_part[...] = expert(1 - c).astype(BF16)
    e_send, e_recv = back_sems
    send(rcopy(expert_part, expert_sib, e_send.at[0, 0], e_recv.at[0, 0], sib))
    rcopy(expert_part, expert_sib, e_send.at[0, 0], e_recv.at[0, 0], sib).wait_recv()
    both = own_out + expert_sib[...].astype(F32)
    for i in range(kv_count):
        x_send[i] = both[:, i * width : (i + 1) * width].astype(BF16)
    for d in range(1, kv_count):
        j = (kv + d) % kv_count
        send(rcopy(x_send.at[j], x_recv.at[kv], e_send.at[1, d], e_recv.at[1, kv], dev_x(j)))
    mine = x_send[kv].astype(F32)
    for d in range(1, kv_count):
        j = (kv + d) % kv_count
        rcopy(x_send.at[j], x_recv.at[j], e_send.at[1, d], e_recv.at[1, j], dev_x(j)).wait_recv()
        mine = mine + x_recv[j].astype(F32)

    back_a[...] = mine.astype(BF16).reshape(back_a.shape)
    for d in far_first(n):
        j = (a + d) % n
        send(rcopy(back_a.at[j], back_mid.at[a], e_send.at[2, d], e_recv.at[2, a], dev_a(j)))
    back_mid[a] = back_a[a]
    for d in near_first(n):
        j = (a + d) % n
        rcopy(back_a.at[j], back_mid.at[j], e_send.at[2, d], e_recv.at[2, j], dev_a(j)).wait_recv()
    back_perm[...] = (
        dot(swap, back_mid[...].reshape(cols, width)).astype(BF16).reshape(back_perm.shape)
    )
    for d in far_first(n):
        j = (b + d) % n
        send(rcopy(back_perm.at[j], back_rows.at[b], e_send.at[3, d], e_recv.at[3, b], dev_b(j)))
    back_rows[b] = back_perm[b]
    for d in near_first(n):
        j = (b + d) % n
        rcopy(
            back_perm.at[j], back_rows.at[j], e_send.at[3, d], e_recv.at[3, j], dev_b(j)
        ).wait_recv()
    returned = back_rows[...].reshape(cols, width)
    combined = dot(share_high, returned) + dot(share_low, returned)
    out_ref[...] = (resid[...].astype(F32) + combined).astype(BF16)
    for copy in sent:
        copy.wait_send()


def local(
    stream_in,
    queries,
    new_kv,
    cache_keys,
    cache_values,
    lengths,
    page_table,
    parents,
    routes,
    norm_gain,
    router,
    gate_w,
    up_w,
    down_w,
):
    kv_count = lax.axis_size("kv")
    n = math.isqrt(lax.axis_size("wide") // 2)
    step_tok, steps, width = queries.shape
    rows = step_tok * steps
    heads = width // HD
    slots = cache_keys.shape[1]
    groups = lengths.shape[0]
    model = router.shape[0]
    units = gate_w.shape[2]
    cols = n * n * MOST
    block = n * MOST
    wide = width + HD
    dma = pltpu.SemaphoreType.DMA
    vmem = pltpu.VMEM
    sems = lambda stages: (dma((stages, max(n, 4))), dma((stages, max(n, 4))))
    in_vmem = pl.BlockSpec(memory_space=pltpu.VMEM)
    in_smem = pl.BlockSpec(memory_space=pltpu.SMEM)
    in_hbm = pl.BlockSpec(memory_space=pl.ANY)
    out = pl.pallas_call(
        functools.partial(kernel, n, kv_count, heads),
        out_shape=jax.ShapeDtypeStruct((rows, width), BF16),
        in_specs=[in_vmem] * 3
        + [in_hbm] * 2
        + [in_smem, in_vmem, in_smem, in_smem, in_vmem]
        + [in_hbm] * 4,
        out_specs=in_vmem,
        scratch_shapes=[
            vmem((slots, BLK, HD), BF16),
            vmem((slots, BLK, HD), BF16),
            vmem(router.shape, BF16),
            vmem((model, units), BF16),
            vmem((model, units), BF16),
            vmem((units, model), BF16),
            dma((8,)),
            vmem((2, n, n, rows, width), BF16),
            vmem((4, rows, 2 * HD), BF16),
            sems(4),
            pltpu.SMEM((slots,), jnp.int32),
            pltpu.SMEM((slots,), jnp.int32),
            pltpu.SMEM((slots,), jnp.int32),
            pltpu.SMEM((groups,), jnp.int32),
            vmem((slots + 1, 4 * rows * heads, 2 * HD), F32),
            vmem((2, n, n, rows, wide), BF16),
            vmem((n, n, rows, wide), BF16),
            vmem((n, n, rows, wide), BF16),
            vmem((n, n, rows, wide), BF16),
            vmem((n, rows, wide), BF16),
            vmem((n, rows, wide), BF16),
            sems(3),
            vmem((rows, width), BF16),
            vmem((kv_count, rows, width), BF16),
            sems(1),
            vmem((n, block, model), BF16),
            vmem((n, block, model), BF16),
            vmem((n, block, model), BF16),
            vmem((2, n, block, model), BF16),
            sems(3),
            vmem((cols, model), BF16),
            vmem((cols, model), BF16),
            vmem((kv_count, cols, width), BF16),
            vmem((kv_count, cols, width), BF16),
            vmem((n, block, width), BF16),
            vmem((n, block, width), BF16),
            vmem((n, block, width), BF16),
            vmem((n, block, width), BF16),
            sems(4),
        ],
        compiler_params=pltpu.CompilerParams(collective_id=0, has_side_effects=True),
        name="layer",
    )(
        stream_in.reshape(rows, width),
        queries.reshape(rows, width),
        new_kv.reshape(rows, 2 * HD),
        cache_keys,
        cache_values,
        lengths,
        page_table,
        parents,
        routes.reshape(rows, routes.shape[2]),
        norm_gain.reshape(1, model),
        router,
        gate_w,
        up_w,
        down_w,
    )
    return out.reshape(step_tok, steps, width)


def solution(mesh):
    return jax.shard_map(
        local,
        mesh=mesh,
        in_specs=(
            P("wide", None, "kv"),
            P("wide", None, "kv"),
            P("wide", None, None, "kv"),
            P("kv", "wide", None, None),
            P("kv", "wide", None, None),
            P(),
            P(),
            P(),
            P("wide", None, None),
            P(),
            P(),
            P("wide", None, "kv"),
            P("wide", None, "kv"),
            P("wide", "kv", None),
        ),
        out_specs=P("wide", None, "kv"),
        check_vma=False,
    )
```

time: 762 us -> 125 us (0.16)
  blocking collectives: 608 us -> 0 us
  Pallas kernels: 0 us -> 110 us
  waiting for transfers between devices: 68 us -> 0 us
  local copies, waits for them, and re-layouts: 49.6 us -> 13 us
  between operations: 13.6 us -> 0.02 us
  starting transfers between devices: 7.81 us -> 0 us
    psum x1 -> x0, blocking collectives: 489 us -> none  [local(): full_num, full_den = lax.psum((part_num, part_den), 'wide')]
    pallas_call x0 -> x1, Pallas kernels: none -> 110 us  [local(): pl.pallas_call(functools.partial(kernel, n, kv_count, heads), out_shape=j...]
    all_gather x2 -> x0, blocking collectives: 68 us -> none  [the longest x1 58.9 us: local(): lax.all_gather(new_kv, 'wide', axis=0, tiled=True)]
    all_to_all x1 -> x0, blocking collectives: 51.2 us -> none  [local(): lax.all_to_all(outgoing, 'wide', split_axis=0, concat_axis=0, tiled=True)]
    all_to_all x1 -> x0, waiting for transfers between devices: 34.8 us -> none  [local(): lax.all_to_all(partial_value.astype(jnp.bfloat16), 'wide', split_axis=0,...]
    unnamed x4 -> x0, waiting for transfers between devices: 20.4 us -> none
    gather x12 -> x0, local copies, waits for them, and re-layouts: 20.1 us -> none  [the longest x6 15.1 us: chain_tokens(): current = group_base + parents[current, earlier - 1]]
    all_gather x1 -> x0, waiting for transfers between devices: 12.7 us -> none  [local(): lax.all_gather(queries, 'wide', axis=0, tiled=True)]
  transfers between devices with their start and end apart: 4 -> 0, of which waited for: 3 -> 0; matrix products, arithmetic and copies ran while one was open for 3% -> 0% of each run, Pallas kernels for 0% -> 0%
where the time goes in v1:
time: 125 us; the launch traced here: 123 us
  Pallas kernels  110 us (88%)
  local copies, waits for them, and re-layouts  13 us (10%)
    pallas_call x1, Pallas kernels, local(): pl.pallas_call(functools.partial(kernel, n, kv_count, heads), out_shape=j...  110 us
    unnamed x9, local copies, waits for them, and re-layouts  7.74 us

profile of v1, /device:TPU:1, one launch (start us, length us, event | category | flops | bytes accessed | tf_op | source)
XLA Modules:
  0.0 123.4 jit_solution(13898037580426075973)
XLA Ops:
  0.0 0.0 copy-start
  0.0 1.4 %copy.21 = bf16[1,8,2,128]{3,1,2,0:T(8,128)(2,1)} copy(bf16[1,8,2,128]{3,2,1,0:T(2,128)(2,1)} %bitcast.7) | data formatting | bytes 8192
  1.4 1.3 %reshape.18.stream_ref = bf16[8,640]{1,0:T(8,128)(2,1)} reshape(bf16[2,4,640]{2,1,0:T(4,128)(2,1)} %param.14) | data formatting | bytes 20480 | tf_op jit(solution)/shard_map/reshape | solution.py:599
  2.7 1.3 %reshape.19.query_ref = bf16[8,640]{1,0:T(8,128)(2,1)} reshape(bf16[2,4,640]{2,1,0:T(4,128)(2,1)} %param.15) | data formatting | bytes 20480 | tf_op jit(solution)/shard_map/reshape | solution.py:600
  4.0 1.3 %reshape.22.gain_ref = f32[1,2560]{1,0:T(1,128)} reshape(f32[2560]{0:T(1024)} %param.23) | data formatting | bytes 20480 | tf_op jit(solution)/shard_map/reshape | solution.py:608
  5.3 1.5 %copy.15.parents_ref = s32[256,3]{1,0:T(8,128)} copy(s32[256,3]{0,1:T(4,128)} %param.21) | data formatting | bytes 6144 | tf_op args[7]
  6.8 2.1 %copy.16.router_hbm = bf16[2560,64]{1,0:T(8,128)(2,1)} copy(bf16[2560,64]{0,1:T(8,128)(2,1)} %param.24) | data formatting | bytes 655360 | tf_op args[10]
  8.8 0.0 copy-done
  8.8 0.0 copy-start.1
  8.8 1.4 %copy.17.gate_hbm = bf16[1,2560,192]{2,1,0:T(8,128)(2,1)} copy(bf16[1,2560,192]{1,2,0:T(8,128)(2,1)S(1)} %copy-done) | data formatting | bytes 1966080 | tf_op args[11]
  10.3 0.0 copy-done.1
  10.3 1.4 %copy.18.up_hbm = bf16[1,2560,192]{2,1,0:T(8,128)(2,1)} copy(bf16[1,2560,192]{1,2,0:T(8,128)(2,1)S(1)} %copy-done.1) | data formatting | bytes 1966080 | tf_op args[12]
  11.7 110.4 %layer.1 = bf16[8,640]{1,0:T(8,128)(2,1)} custom-call(bf16[8,640]{1,0:T(8,128)(2,1)} %reshape.18.stream_ref, bf16[8,640]{1,0:T(8,128)(2,1)} %reshape.19.query_ref, bf16[8,256]{1,0:T(8,128)(2,1)} %bitcast.6, bf16[1,16,128,128]{3,2,1,0:T(8,128)(2,1)} %keys_hbm.1, bf16[1,16,128,128]{3,2,1,0:T(8,128)(2,1)} %values_hbm.1, s32[32]{0:T(128)} %lengths_ref.1, ...), custom_call_target="tpu_custom_call" | custom-call | tf_op jit(solution)/shard_map/layer/pallas_call | solution.py:547
  122.1 1.3 %reshape.23 = bf16[2,4,640]{2,1,0:T(4,128)(2,1)} reshape(bf16[8,640]{1,0:T(8,128)(2,1)} %layer.1) | data formatting | bytes 20480 | tf_op jit(solution)/shard_map/reshape | solution.py:614
Async XLA Ops:
  0.0 8.8 %copy-start = (bf16[1,2560,192]{1,2,0:T(8,128)(2,1)S(1)}, bf16[1,2560,192]{1,2,0:T(8,128)(2,1)}, u32[]{:S(2)}) copy-start(bf16[1,2560,192]{1,2,0:T(8,128)(2,1)} %param.25) | copy-start | bytes 2949124
  8.8 1.4 %copy-start.1 = (bf16[1,2560,192]{1,2,0:T(8,128)(2,1)S(1)}, bf16[1,2560,192]{1,2,0:T(8,128)(2,1)}, u32[]{:S(2)}) copy-start(bf16[1,2560,192]{1,2,0:T(8,128)(2,1)} %param.26) | copy-start | bytes 2949124

commit v2 on v1

v2 whole, which is shorter than its diff:
```python
import functools
import math

import jax
import jax.numpy as jnp
from jax import lax
from jax.experimental import pallas as pl
from jax.experimental.pallas import tpu as pltpu
from jax.sharding import PartitionSpec as P

MESH = pl.DeviceIdType.MESH
HD = 128
BEAMS = 8
BLK = 128
MOST = 2
F32 = jnp.float32
BF16 = jnp.bfloat16


def far_first(n):
    order = sorted(range(1, n), key=lambda d: -min(d, n - d))
    return order


def near_first(n):
    return sorted(range(1, n), key=lambda d: min(d, n - d))


def rcopy(src, dst, send_sem, recv_sem, device):
    return pltpu.make_async_remote_copy(
        src_ref=src,
        dst_ref=dst,
        send_sem=send_sem,
        recv_sem=recv_sem,
        device_id=device,
        device_id_type=MESH,
    )


def dot(x, y):
    return jnp.dot(x, y, preferred_element_type=F32)


def iota(shape, axis):
    return lax.broadcasted_iota(jnp.int32, shape, axis)


def kernel(
    n,
    kv_count,
    heads,
    stream_ref,
    query_ref,
    newkv_ref,
    keys_hbm,
    values_hbm,
    lengths_ref,
    table_ref,
    parents_ref,
    routes_ref,
    gain_hbm,
    router_hbm,
    gate_hbm,
    up_hbm,
    down_hbm,
    out_ref,
    keys,
    values,
    router,
    gate,
    up,
    down,
    gain,
    load_sem,
    query,
    qfull,
    kvgroup,
    routes_b,
    q_sems,
    slot_group,
    slot_limit,
    slot_prev,
    group_last,
    sums,
    part,
    sibling_part,
    core_sum,
    b_parts,
    b_sum,
    a_parts,
    part_sems,
    resid,
    resid_all,
    x_sems,
    normed_own,
    mid_rows,
    mid_perm,
    rows,
    row_sems,
    expert_part,
    expert_sib,
    x_send,
    x_recv,
    back_a,
    back_mid,
    back_sum,
    back_rows,
    back_sems,
):
    kv = lax.axis_index("kv")
    w = lax.axis_index("wide")
    c = w % 2
    z = (w // 2) % n
    y = w // (2 * n)
    a = z + c * (y - z)
    b = y + c * (z - y)
    stride_a = 2 + c * (2 * n - 2)
    stride_b = 2 * n - c * (2 * n - 2)
    sib = {"wide": w + 1 - 2 * c}
    width = heads * HD
    row_count = query.shape[0]
    slots = keys.shape[0]
    groups = lengths_ref.shape[0]
    blocks = table_ref.shape[1]
    steps = parents_ref.shape[0] + 1
    top = routes_ref.shape[1]
    model = kv_count * width
    cols = n * n * MOST
    block_rows = n * MOST
    mids = n * row_count
    scale = 1.0 / math.sqrt(HD)

    def dev_a(j):
        return {"wide": w + (j - a) * stride_a}

    def dev_b(j):
        return {"wide": w + (j - b) * stride_b}

    def dev_x(j):
        return {"kv": j}

    group_first = w // 4 * 4
    group_place = w % 4

    loads = [
        pltpu.make_async_copy(src, dst, load_sem.at[i])
        for i, (src, dst) in enumerate(
            [
                (keys_hbm.at[0], keys),
                (values_hbm.at[0], values),
                (router_hbm, router),
                (gate_hbm.at[0], gate),
                (up_hbm.at[0], up),
                (gain_hbm, gain.at[0]),
            ]
            + [
                (down_hbm.at[0, :, i * width : (i + 1) * width], down.at[i])
                for i in range(kv_count)
            ]
        )
    ]
    for load in loads:
        load.start()
    query[...] = query_ref[...].reshape(query.shape)
    qfull[c, b, a] = query[...]
    kvgroup[group_place] = newkv_ref[...].reshape(row_count, 2 * HD)
    routes_b[b] = routes_ref[...]

    barrier = pltpu.get_barrier_semaphore()
    greeted = 0
    for d in far_first(n):
        for device in (dev_a((a + d) % n), dev_b((b + d) % n)):
            pl.semaphore_signal(barrier, inc=1, device_id=device, device_id_type=MESH)
            greeted += 1
    for d in range(1, kv_count):
        pl.semaphore_signal(
            barrier, inc=1, device_id=dev_x((kv + d) % kv_count), device_id_type=MESH
        )
        greeted += 1
    for d in range(1, 4):
        pl.semaphore_signal(
            barrier,
            inc=1,
            device_id={"wide": group_first + (group_place + d) % 4},
            device_id_type=MESH,
        )
        greeted += 1
    pl.semaphore_wait(barrier, greeted)

    sent = []

    def send(copy):
        copy.start()
        sent.append(copy)

    q_send, q_recv = q_sems
    for d in far_first(n):
        send(
            rcopy(query, qfull.at[c, b, a], q_send.at[0, d], q_recv.at[0, a], dev_a((a + d) % n))
        )
    for d in range(1, 4):
        peer = group_first + (group_place + d) % 4
        send(
            rcopy(
                kvgroup.at[group_place],
                kvgroup.at[group_place],
                q_send.at[3, d],
                q_recv.at[3, group_place],
                {"wide": peer},
            )
        )

    for d in near_first(n):
        j = (a + d) % n
        rcopy(query, qfull.at[c, b, j], q_send.at[0, d], q_recv.at[0, j], dev_a(j)).wait_recv()
    for d in far_first(n):
        send(
            rcopy(
                qfull.at[c, b],
                qfull.at[c, b],
                q_send.at[1, d],
                q_recv.at[1, b],
                dev_b((b + d) % n),
            )
        )
    send(rcopy(qfull.at[c, b], qfull.at[c, b], q_send.at[2, 0], q_recv.at[2, b], sib))
    for d in far_first(n):
        send(
            rcopy(
                routes_b.at[b],
                routes_b.at[b],
                q_send.at[4, d],
                q_recv.at[4, b],
                dev_b((b + d) % n),
            )
        )

    table = table_ref[...]
    place = iota((groups, blocks), 0) * blocks + iota((groups, blocks), 1) + 1
    owners = []
    for s in range(slots):
        code = jnp.max(jnp.where(table == w * slots + s, place, 0))
        live = jnp.minimum(code, 1)
        spot = jnp.maximum(code - 1, 0)
        group = spot // blocks
        slot_group[s] = group
        slot_limit[s] = live * (lengths_ref[group] - spot % blocks * BLK)
        owners.append(jnp.where(code > 0, group, -1))
    for s in range(slots):
        before = jnp.int32(slots)
        for r in range(s):
            before = jnp.where(owners[r] == owners[s], r, before)
        slot_prev[s] = before
    for g in range(groups):
        last = jnp.int32(slots)
        for s in range(slots):
            last = jnp.where(owners[s] == g, s, last)
        group_last[g] = last
    sums[slots] = jnp.zeros(sums.shape[1:], F32)

    for d in near_first(n):
        j = (b + d) % n
        rcopy(
            qfull.at[c, b], qfull.at[c, j], q_send.at[1, d], q_recv.at[1, j], dev_b(j)
        ).wait_recv()
        send(rcopy(qfull.at[c, j], qfull.at[c, j], q_send.at[2, d], q_recv.at[2, j], sib))
    for j in range(n):
        rcopy(
            qfull.at[1 - c, j], qfull.at[1 - c, j], q_send.at[2, j], q_recv.at[2, j], sib
        ).wait_recv()

    loads[0].wait()
    loads[1].wait()
    half_n = n // 2
    group_rows = 4 * row_count

    def one_slot(s):
        group = slot_group[s]
        gy = group // half_n
        gz = group % half_n * 2
        q = jnp.concatenate(
            [qfull[0, gy, gz], qfull[0, gy, gz + 1], qfull[1, gz, gy], qfull[1, gz + 1, gy]],
            axis=0,
        )
        q = jnp.concatenate([q[:, r * HD : (r + 1) * HD] for r in range(heads)], axis=0)
        scores = lax.dot_general(
            q, keys[s], (((1,), (1,)), ((), ())), preferred_element_type=F32
        )
        ok = iota(scores.shape, 1) < slot_limit[s]
        weights = jnp.where(ok, jnp.exp(scores * scale), 0.0).astype(BF16)
        extended = jnp.concatenate([values[s], jnp.ones((BLK, HD), BF16)], axis=1)
        sums[s] = dot(weights, extended)

    def slot_block(s, carry):
        for i in range(4):
            one_slot(s * 4 + i)
        return carry

    lax.fori_loop(0, slots // 4, slot_block, 0)

    def link_slot(s, carry):
        sums[s] = sums[s] + sums[slot_prev[s]]
        return carry

    lax.fori_loop(0, slots, link_slot, 0)

    lane = iota((row_count, HD), 1)
    tiles = n * heads
    for core in range(2):
        for j in range(n):
            part[core, j, tiles] = jnp.zeros((row_count, HD), BF16)

    def one_group(g, carry):
        last = group_last[g]
        gy = g // half_n
        gz = g % half_n * 2
        for core in range(2):
            for zl in range(2):
                bi, ai = (gy, gz + zl) if core == 0 else (gz + zl, gy)
                dens = jnp.zeros((row_count, HD), F32)
                for r in range(heads):
                    first = r * group_rows + (core * 2 + zl) * row_count
                    block = sums[last, pl.ds(first, row_count), :]
                    part[core, bi, ai * heads + r] = block[:, :HD].astype(BF16)
                    dens = jnp.where(lane % 8 == r, block[:, HD:], dens)
                old = part[core, bi, tiles].astype(F32)
                part[core, bi, tiles] = jnp.where(lane // 8 == ai, dens, old).astype(BF16)
        return carry

    lax.fori_loop(0, groups, one_group, 0)

    p_send, p_recv = part_sems
    for d in far_first(n) + [0]:
        j = (a + d) % n
        send(rcopy(part.at[1 - c, j], sibling_part.at[j], p_send.at[0, d], p_recv.at[0, j], sib))
    for d in far_first(n) + [0]:
        j = (b + d) % n
        rcopy(
            part.at[1 - c, j], sibling_part.at[j], p_send.at[0, d], p_recv.at[0, j], sib
        ).wait_recv()
        core_sum[j] = (part[c, j].astype(F32) + sibling_part[j].astype(F32)).astype(BF16)
        if d:
            send(rcopy(core_sum.at[j], b_parts.at[b], p_send.at[1, d], p_recv.at[1, b], dev_b(j)))

    for j in range(1, 4):
        p = (group_place + j) % 4
        rcopy(
            kvgroup.at[p], kvgroup.at[p], q_send.at[3, j], q_recv.at[3, p], {"wide": group_first + p}
        ).wait_recv()
    key_rows = 4 * row_count
    tail_kv = jnp.concatenate([kvgroup[i] for i in range(4)], axis=0)
    row_id = iota((row_count, key_rows), 0)
    key_id = iota((row_count, key_rows), 1)
    wanted = jnp.full((row_count, key_rows), -1, jnp.int32)
    token_base = w // 4 * BEAMS
    for i in range(row_count // steps):
        for s in range(steps):
            beam = group_place * (row_count // steps) + i
            for j in range(s, -1, -1):
                wanted = jnp.where(
                    (row_id == i * steps + s) & (key_id % steps == j), beam, wanted
                )
                if j:
                    beam = parents_ref[j - 1, token_base + beam]
    allowed = wanted == key_id // steps
    tail_q = jnp.concatenate([query[:, r * HD : (r + 1) * HD] for r in range(heads)], axis=0)
    tail_scores = lax.dot_general(
        tail_q, tail_kv[:, :HD], (((1,), (1,)), ((), ())), preferred_element_type=F32
    )
    tail_ok = jnp.concatenate([allowed.astype(F32)] * heads, axis=0)
    tail_w = jnp.where(tail_ok > 0, jnp.exp(tail_scores * scale), 0.0).astype(BF16)
    tail_num = dot(tail_w, tail_kv[:, HD:])
    tail_den = jnp.sum(tail_w.astype(F32), axis=1, keepdims=True)

    for d in near_first(n):
        j = (b + d) % n
        rcopy(
            routes_b.at[j], routes_b.at[j], q_send.at[4, d], q_recv.at[4, j], dev_b(j)
        ).wait_recv()
    routed = jnp.concatenate([routes_b[j] for j in range(n)], axis=0)
    col = iota((1, cols), 1)
    col_chip = col // block_rows
    col_source = col // MOST % n
    col_place = col % MOST
    col_expert = b * n + col_chip + c * ((col_chip - b) * (n - 1))
    experts = n * n
    source = iota((mids, 1), 0) // row_count
    expert_lane = iota((1, experts), 1)
    hit = jnp.zeros((mids, cols), F32)
    chosen = jnp.zeros((mids, experts), F32)
    for i in range(top):
        hit = jnp.where(routed[:, i : i + 1] == col_expert, 1.0, hit)
        chosen = jnp.where(routed[:, i : i + 1] == expert_lane, 1.0, chosen)
    hit = jnp.where(source == col_source, hit, 0.0)
    first_id = iota((mids, mids), 0)
    second_id = iota((mids, mids), 1)
    earlier = (first_id > second_id) & (first_id // row_count == second_id // row_count)
    taken = dot(earlier.astype(F32).astype(BF16), hit.astype(BF16))
    pick = jnp.where(taken == col_place.astype(F32), hit, 0.0)
    pick_t = jnp.transpose(pick).astype(BF16)
    spread = (iota((experts, cols), 0) == col_expert).astype(F32)

    for d in near_first(n):
        j = (b + d) % n
        rcopy(core_sum.at[j], b_parts.at[j], p_send.at[1, d], p_recv.at[1, j], dev_b(j)).wait_recv()
    dens = core_sum[b, tiles].astype(F32)
    for e in range(1, n):
        dens = dens + b_parts[(b + e) % n, tiles].astype(F32)
    dens = dens.astype(BF16)
    for d in far_first(n) + [0]:
        j = (a + d) % n
        chunk = pl.ds(j * heads, heads)
        total = core_sum[b, chunk].astype(F32)
        for e in range(1, n):
            total = total + b_parts[(b + e) % n, chunk].astype(F32)
        b_sum[j, 0:heads] = total.astype(BF16)
        b_sum[j, heads] = dens
        if d:
            send(rcopy(b_sum.at[j], a_parts.at[a], p_send.at[2, d], p_recv.at[2, a], dev_a(j)))
    total = b_sum[a].astype(F32)
    for d in near_first(n):
        j = (a + d) % n
        rcopy(b_sum.at[j], a_parts.at[j], p_send.at[2, d], p_recv.at[2, j], dev_a(j)).wait_recv()
        total = total + a_parts[j].astype(F32)

    attended = []
    for r in range(heads):
        num = total[r] + tail_num[r * row_count : (r + 1) * row_count]
        mine = jnp.sum(jnp.where(lane == a * 8 + r, total[heads], 0.0), axis=1, keepdims=True)
        den = mine + tail_den[r * row_count : (r + 1) * row_count]
        attended.append((num / den).astype(BF16).astype(F32))
    residual = (stream_ref[...].reshape(row_count, width).astype(F32) + jnp.concatenate(attended, axis=1)).astype(BF16)
    resid[...] = residual

    x_ssem, x_rsem = x_sems
    for d in range(1, kv_count):
        send(
            rcopy(
                resid, resid_all.at[kv], x_ssem.at[0, d], x_rsem.at[0, kv], dev_x((kv + d) % kv_count)
            )
        )
    resid_all[kv] = residual
    loads[2].wait()
    loads[5].wait()
    for d in range(1, kv_count):
        j = (kv + d) % kv_count
        rcopy(resid, resid_all.at[j], x_ssem.at[0, d], x_rsem.at[0, j], dev_x(j)).wait_recv()
    full = jnp.concatenate([resid_all[i].astype(F32) for i in range(kv_count)], axis=1)
    mean_square = jnp.sum(full * full, axis=1, keepdims=True) / full.shape[1]
    normed = (full * lax.rsqrt(mean_square + 1e-06) * gain[...]).astype(BF16)

    r_send, r_recv = row_sems
    normed_own[...] = normed
    for d in far_first(n):
        j = (b + d) % n
        send(rcopy(normed_own, mid_rows.at[b], r_send.at[0, d], r_recv.at[0, b], dev_b(j)))
    mid_rows[b] = normed
    for d in near_first(n):
        j = (b + d) % n
        rcopy(normed_own, mid_rows.at[j], r_send.at[0, d], r_recv.at[0, j], dev_b(j)).wait_recv()
    mid = jnp.concatenate([mid_rows[j] for j in range(n)], axis=0)
    mid_perm[...] = dot(pick_t, mid).astype(BF16).reshape(mid_perm.shape)
    for d in far_first(n):
        j = (a + d) % n
        send(rcopy(mid_perm.at[j], rows.at[c, a], r_send.at[1, d], r_recv.at[1, a], dev_a(j)))
    send(rcopy(mid_perm.at[a], rows.at[c, a], r_send.at[2, 0], r_recv.at[2, a], sib))
    rows[c, a] = mid_perm[a]

    logits = lax.dot_general(
        mid, router[...], (((1,), (1,)), ((), ())), preferred_element_type=F32
    )
    col_logits = lax.dot_general(
        logits,
        spread,
        (((1,), (0,)), ((), ())),
        preferred_element_type=F32,
        precision=lax.Precision.HIGHEST,
    )
    raised = jnp.where(chosen > 0, jnp.exp(jnp.where(chosen > 0, logits, 0.0)), 0.0)
    raised_sum = jnp.sum(raised, axis=1, keepdims=True)
    share = jnp.where(pick > 0, jnp.exp(jnp.where(pick > 0, col_logits, 0.0)), 0.0) / raised_sum
    share_high = share.astype(BF16)
    share_low = (share - share_high.astype(F32)).astype(BF16)

    for d in near_first(n):
        j = (a + d) % n
        rcopy(mid_perm.at[j], rows.at[c, j], r_send.at[1, d], r_recv.at[1, j], dev_a(j)).wait_recv()
        send(rcopy(rows.at[c, j], rows.at[c, j], r_send.at[2, d], r_recv.at[2, j], sib))
    loads[3].wait()
    loads[4].wait()

    def hidden(core):
        x = rows[core].reshape(cols, model)
        gated = lax.dot_general(
            x, gate[...], (((1,), (1,)), ((), ())), preferred_element_type=F32
        )
        lifted = lax.dot_general(
            x, up[...], (((1,), (1,)), ((), ())), preferred_element_type=F32
        )
        return (gated / (1.0 + jnp.exp(-gated)) * lifted).astype(BF16)

    own_hidden = hidden(c)
    for j in range(n):
        rcopy(
            rows.at[1 - c, j], rows.at[1 - c, j], r_send.at[2, j], r_recv.at[2, j], sib
        ).wait_recv()
    sib_hidden = hidden(1 - c)
    for load in loads[6:]:
        load.wait()
    e_send, e_recv = back_sems
    slices = far_first(kv_count) + [0]
    for d in slices:
        i = (kv + d) % kv_count
        expert_part[i] = dot(sib_hidden, down[i]).astype(BF16)
        send(rcopy(expert_part.at[i], expert_sib.at[i], e_send.at[0, d], e_recv.at[0, i], sib))
    for d in slices:
        i = (kv + d) % kv_count
        own_out = dot(own_hidden, down[i])
        rcopy(
            expert_part.at[i], expert_sib.at[i], e_send.at[0, d], e_recv.at[0, i], sib
        ).wait_recv()
        both = own_out + expert_sib[i].astype(F32)
        if d:
            x_send[i] = both.astype(BF16)
            send(rcopy(x_send.at[i], x_recv.at[kv], e_send.at[1, d], e_recv.at[1, kv], dev_x(i)))
    mine = both
    for d in range(1, kv_count):
        j = (kv + d) % kv_count
        rcopy(x_send.at[j], x_recv.at[j], e_send.at[1, d], e_recv.at[1, j], dev_x(j)).wait_recv()
        mine = mine + x_recv[j].astype(F32)

    back_a[...] = mine.astype(BF16).reshape(back_a.shape)
    for d in far_first(n):
        j = (a + d) % n
        send(rcopy(back_a.at[j], back_mid.at[a], e_send.at[2, d], e_recv.at[2, a], dev_a(j)))
    back_mid[a] = back_a[a]
    for d in near_first(n):
        j = (a + d) % n
        rcopy(back_a.at[j], back_mid.at[j], e_send.at[2, d], e_recv.at[2, j], dev_a(j)).wait_recv()
    returned = back_mid[...].reshape(cols, width)
    weighted = dot(share_high, returned) + dot(share_low, returned)
    back_sum[...] = weighted.astype(BF16).reshape(back_sum.shape)
    for d in far_first(n):
        j = (b + d) % n
        send(rcopy(back_sum.at[j], back_rows.at[b], e_send.at[3, d], e_recv.at[3, b], dev_b(j)))
    combined = resid[...].astype(F32) + back_sum[b].astype(F32)
    for d in near_first(n):
        j = (b + d) % n
        rcopy(
            back_sum.at[j], back_rows.at[j], e_send.at[3, d], e_recv.at[3, j], dev_b(j)
        ).wait_recv()
        combined = combined + back_rows[j].astype(F32)
    out_ref[...] = combined.astype(BF16).reshape(out_ref.shape)
    for copy in sent:
        copy.wait_send()


def local(
    stream_in,
    queries,
    new_kv,
    cache_keys,
    cache_values,
    lengths,
    page_table,
    parents,
    routes,
    norm_gain,
    router,
    gate_w,
    up_w,
    down_w,
):
    kv_count = lax.axis_size("kv")
    n = math.isqrt(lax.axis_size("wide") // 2)
    step_tok, steps, width = queries.shape
    rows = step_tok * steps
    heads = width // HD
    slots = cache_keys.shape[1]
    groups = lengths.shape[0]
    model = router.shape[0]
    units = gate_w.shape[2]
    cols = n * n * MOST
    block = n * MOST
    tiles = n * heads + 1
    dma = pltpu.SemaphoreType.DMA
    vmem = pltpu.VMEM
    sems = lambda stages: (dma((stages, max(n, 4))), dma((stages, max(n, 4))))
    in_vmem = pl.BlockSpec(memory_space=pltpu.VMEM)
    in_smem = pl.BlockSpec(memory_space=pltpu.SMEM)
    in_hbm = pl.BlockSpec(memory_space=pl.ANY)
    return pl.pallas_call(
        functools.partial(kernel, n, kv_count, heads),
        out_shape=jax.ShapeDtypeStruct(stream_in.shape, BF16),
        in_specs=[in_vmem] * 3
        + [in_hbm] * 2
        + [in_smem, in_vmem, in_smem, in_vmem]
        + [in_hbm] * 5,
        out_specs=in_vmem,
        scratch_shapes=[
            vmem((slots, BLK, HD), BF16),
            vmem((slots, BLK, HD), BF16),
            vmem((router.shape[1], model), BF16),
            vmem((units, model), BF16),
            vmem((units, model), BF16),
            vmem((kv_count, units, width), BF16),
            vmem((1, model), F32),
            dma((6 + kv_count,)),
            vmem((rows, width), BF16),
            vmem((2, n, n, rows, width), BF16),
            vmem((4, rows, 2 * HD), BF16),
            vmem((n, rows, routes.shape[2]), jnp.int32),
            sems(5),
            pltpu.SMEM((slots,), jnp.int32),
            pltpu.SMEM((slots,), jnp.int32),
            pltpu.SMEM((slots,), jnp.int32),
            pltpu.SMEM((groups,), jnp.int32),
            vmem((slots + 1, 4 * rows * heads, 2 * HD), F32),
            vmem((2, n, tiles, rows, HD), BF16),
            vmem((n, tiles, rows, HD), BF16),
            vmem((n, tiles, rows, HD), BF16),
            vmem((n, tiles, rows, HD), BF16),
            vmem((n, heads + 1, rows, HD), BF16),
            vmem((n, heads + 1, rows, HD), BF16),
            sems(3),
            vmem((rows, width), BF16),
            vmem((kv_count, rows, width), BF16),
            sems(1),
            vmem((rows, model), BF16),
            vmem((n, rows, model), BF16),
            vmem((n, block, model), BF16),
            vmem((2, n, block, model), BF16),
            sems(3),
            vmem((kv_count, cols, width), BF16),
            vmem((kv_count, cols, width), BF16),
            vmem((kv_count, cols, width), BF16),
            vmem((kv_count, cols, width), BF16),
            vmem((n, block, width), BF16),
            vmem((n, block, width), BF16),
            vmem((n, rows, width), BF16),
            vmem((n, rows, width), BF16),
            sems(4),
        ],
        compiler_params=pltpu.CompilerParams(collective_id=0, has_side_effects=True),
        name="layer",
    )(
        stream_in,
        queries,
        new_kv,
        cache_keys,
        cache_values,
        lengths,
        page_table,
        jnp.swapaxes(parents, 0, 1),
        routes.reshape(rows, routes.shape[2]),
        norm_gain,
        jnp.swapaxes(router, 0, 1),
        jnp.swapaxes(gate_w, 1, 2),
        jnp.swapaxes(up_w, 1, 2),
        down_w,
    )


def solution(mesh):
    return jax.shard_map(
        local,
        mesh=mesh,
        in_specs=(
            P("wide", None, "kv"),
            P("wide", None, "kv"),
            P("wide", None, None, "kv"),
            P("kv", "wide", None, None),
            P("kv", "wide", None, None),
            P(),
            P(),
            P(),
            P("wide", None, None),
            P(),
            P(),
            P("wide", None, "kv"),
            P("wide", None, "kv"),
            P("wide", "kv", None),
        ),
        out_specs=P("wide", None, "kv"),
        check_vma=False,
    )
```

time: 125 us -> 103 us (0.82)
  local copies, waits for them, and re-layouts: 13 us -> 1.31 us
  Pallas kernels: 110 us -> 101 us
    pallas_call x1, Pallas kernels: 110 us -> 101 us  [local(): pl.pallas_call(functools.partial(kernel, n, kv_count, heads), out_shape=j...]
    unnamed x9 -> x1, local copies, waits for them, and re-layouts: 7.74 us -> 1.31 us
    reshape x4 -> x0, local copies, waits for them, and re-layouts: 5.23 us -> none  [the longest x1 1.31 us: local(): return out.reshape(step_tok, steps, width)]
where the time goes in v2:
time: 103 us; the launch traced here: 102 us
  Pallas kernels  101 us (98%)
  local copies, waits for them, and re-layouts  1.31 us (1%)
    pallas_call x1, Pallas kernels, local(): pl.pallas_call(functools.partial(kernel, n, kv_count, heads), out_shape=j...  101 us

profile of v2, /device:TPU:1, one launch (start us, length us, event | category | flops | bytes accessed | tf_op | source)
XLA Modules:
  0.0 101.9 jit_solution(488534928311823820)
XLA Ops:
  0.0 100.6 %layer.1 = bf16[2,4,640]{2,1,0:T(4,128)(2,1)} custom-call(bf16[2,4,640]{2,1,0:T(4,128)(2,1)} %stream_ref.1, bf16[2,4,640]{2,1,0:T(4,128)(2,1)} %query_ref.1, bf16[2,4,2,128]{3,2,1,0:T(2,128)(2,1)} %newkv_ref.1, bf16[1,16,128,128]{3,2,1,0:T(8,128)(2,1)} %keys_hbm.1, bf16[1,16,128,128]{3,2,1,0:T(8,128)(2,1)} %values_hbm.1, s32[32]{0:T(128)} %lengths_ref.1, ...), custom_call_target="tpu_custom_call" | custom-call | tf_op jit(solution)/shard_map/layer/pallas_call | solution.py:592
  100.6 1.3 %copy.16 = bf16[2,4,640]{2,1,0:T(4,128)(2,1)} copy(bf16[2,4,640]{2,1,0:T(4,128)(2,1)} %layer.1) | data formatting | bytes 20480

commit v3 on v2

--- a/solution.py
+++ b/solution.py
@@ -73,7 +73,8 @@
     gain,
     load_sem,
     query,
-    qfull,
+    query_parts,
+    q_all,
     kvgroup,
     routes_b,
     q_sems,
@@ -81,27 +82,23 @@
     slot_limit,
     slot_prev,
     group_last,
-    sums,
-    part,
+    sums_all,
+    part_all,
     sibling_part,
-    core_sum,
+    core_sum_all,
     b_parts,
     b_sum,
     a_parts,
     part_sems,
     resid,
-    resid_all,
+    mid_resid,
     x_sems,
-    normed_own,
-    mid_rows,
     mid_perm,
     rows,
     row_sems,
     expert_part,
     expert_sib,
     x_send,
-    x_recv,
-    back_a,
     back_mid,
     back_sum,
     back_rows,
@@ -136,8 +133,13 @@
     def dev_b(j):
         return {"wide": w + (j - b) * stride_b}
 
-    def dev_x(j):
-        return {"kv": j}
+    def dev_xa(i, j):
+        return {"kv": i, "wide": w + (j - a) * stride_a}
+
+    def dev_xb(i, j):
+        return {"kv": i, "wide": w + (j - b) * stride_b}
+
+    spans = [(0, (heads + 1) // 2), ((heads + 1) // 2, heads)]
 
     group_first = w // 4 * 4
     group_place = w % 4
@@ -162,21 +164,23 @@
     for load in loads:
         load.start()
     query[...] = query_ref[...].reshape(query.shape)
-    qfull[c, b, a] = query[...]
+    for (first, last), share_q, all_q in zip(spans, query_parts, q_all):
+        share_q[...] = query[:, first * HD : last * HD]
+        all_q[c, b, a] = share_q[...]
     kvgroup[group_place] = newkv_ref[...].reshape(row_count, 2 * HD)
     routes_b[b] = routes_ref[...]
 
     barrier = pltpu.get_barrier_semaphore()
     greeted = 0
-    for d in far_first(n):
-        for device in (dev_a((a + d) % n), dev_b((b + d) % n)):
+    line = far_first(n)
+    for dx in range(kv_count):
+        i = (kv + dx) % kv_count
+        devices = [dev_xa(i, (a + d) % n) for d in line] + [dev_xb(i, (b + d) % n) for d in line]
+        if dx:
+            devices.append(dev_xa(i, a))
+        for device in devices:
             pl.semaphore_signal(barrier, inc=1, device_id=device, device_id_type=MESH)
             greeted += 1
-    for d in range(1, kv_count):
-        pl.semaphore_signal(
-            barrier, inc=1, device_id=dev_x((kv + d) % kv_count), device_id_type=MESH
-        )
-        greeted += 1
     for d in range(1, 4):
         pl.semaphore_signal(
             barrier,
@@ -194,10 +198,17 @@
         sent.append(copy)
 
     q_send, q_recv = q_sems
-    for d in far_first(n):
-        send(
-            rcopy(query, qfull.at[c, b, a], q_send.at[0, d], q_recv.at[0, a], dev_a((a + d) % n))
-        )
+    for ch, share_q in enumerate(query_parts):
+        for d in far_first(n):
+            send(
+                rcopy(
+                    share_q,
+                    q_all[ch].at[c, b, a],
+                    q_send.at[7 * ch, d],
+                    q_recv.at[7 * ch, a],
+                    dev_a((a + d) % n),
+                )
+            )
     for d in range(1, 4):
         peer = group_first + (group_place + d) % 4
         send(
@@ -210,20 +221,20 @@
             )
         )
 
-    for d in near_first(n):
-        j = (a + d) % n
-        rcopy(query, qfull.at[c, b, j], q_send.at[0, d], q_recv.at[0, j], dev_a(j)).wait_recv()
-    for d in far_first(n):
-        send(
-            rcopy(
-                qfull.at[c, b],
-                qfull.at[c, b],
-                q_send.at[1, d],
-                q_recv.at[1, b],
-                dev_b((b + d) % n),
+    for ch in range(2):
+        for d in near_first(n):
+            j = (a + d) % n
+            rcopy(
+                query_parts[ch], q_all[ch].at[c, b, j], q_send.at[7 * ch, d], q_recv.at[7 * ch, j], dev_a(j)
+            ).wait_recv()
+        block = q_all[ch].at[c, b]
+        for d in far_first(n):
+            send(
+                rcopy(
+                    block, block, q_send.at[1 + 4 * ch, d], q_recv.at[1 + 4 * ch, b], dev_b((b + d) % n)
+                )
             )
-        )
-    send(rcopy(qfull.at[c, b], qfull.at[c, b], q_send.at[2, 0], q_recv.at[2, b], sib))
+        send(rcopy(block, block, q_send.at[2 + 4 * ch, 0], q_recv.at[2 + 4 * ch, b], sib))
     for d in far_first(n):
         send(
             rcopy(
@@ -256,91 +267,138 @@
         for s in range(slots):
             last = jnp.where(owners[s] == g, s, last)
         group_last[g] = last
-    sums[slots] = jnp.zeros(sums.shape[1:], F32)
-
-    for d in near_first(n):
-        j = (b + d) % n
-        rcopy(
-            qfull.at[c, b], qfull.at[c, j], q_send.at[1, d], q_recv.at[1, j], dev_b(j)
-        ).wait_recv()
-        send(rcopy(qfull.at[c, j], qfull.at[c, j], q_send.at[2, d], q_recv.at[2, j], sib))
-    for j in range(n):
-        rcopy(
-            qfull.at[1 - c, j], qfull.at[1 - c, j], q_send.at[2, j], q_recv.at[2, j], sib
-        ).wait_recv()
-
+
+    def pass_on(ch):
+        for d in near_first(n):
+            j = (b + d) % n
+            block = q_all[ch].at[c, j]
+            rcopy(
+                block, block, q_send.at[1 + 4 * ch, d], q_recv.at[1 + 4 * ch, j], dev_b(j)
+            ).wait_recv()
+            send(rcopy(block, block, q_send.at[2 + 4 * ch, d], q_recv.at[2 + 4 * ch, j], sib))
+
+    def await_sibling(ch):
+        for j in range(n):
+            block = q_all[ch].at[1 - c, j]
+            rcopy(
+                block, block, q_send.at[2 + 4 * ch, j], q_recv.at[2 + 4 * ch, j], sib
+            ).wait_recv()
+
+    half_n = n // 2
+    group_rows = 4 * row_count
+    lane = iota((row_count, HD), 1)
+    p_send, p_recv = part_sems
+
+    def attend(ch):
+        first_head, last_head = spans[ch]
+        count = last_head - first_head
+        sums, part = sums_all[ch], part_all[ch]
+        tiles = n * count
+        qfull = q_all[ch]
+
+        def one_slot(s):
+            group = slot_group[s]
+            gy = group // half_n
+            gz = group % half_n * 2
+            q = jnp.concatenate(
+                [
+                    qfull[0, gy, gz],
+                    qfull[0, gy, gz + 1],
+                    qfull[1, gz, gy],
+                    qfull[1, gz + 1, gy],
+                ],
+                axis=0,
+            )
+            q = jnp.concatenate([q[:, r * HD : (r + 1) * HD] for r in range(count)], axis=0)
+            scores = lax.dot_general(
+                q, keys[s], (((1,), (1,)), ((), ())), preferred_element_type=F32
+            )
+            ok = iota(scores.shape, 1) < slot_limit[s]
+            weights = jnp.where(ok, jnp.exp(scores * scale), 0.0).astype(BF16)
+            extended = jnp.concatenate([values[s], jnp.ones((BLK, HD), BF16)], axis=1)
+            sums[s] = dot(weights, extended)
+
+        def slot_block(s, carry):
+            for i in range(4):
+                one_slot(s * 4 + i)
+            return carry
+
+        sums[slots] = jnp.zeros(sums.shape[1:], F32)
+        lax.fori_loop(0, slots // 4, slot_block, 0)
+
+        def link_slot(s, carry):
+            sums[s] = sums[s] + sums[slot_prev[s]]
+            return carry
+
+        lax.fori_loop(0, slots, link_slot, 0)
+
+        for core in range(2):
+            for j in range(n):
+                part[core, j, tiles] = jnp.zeros((row_count, HD), BF16)
+
+        def one_group(g, carry):
+            last = group_last[g]
+            gy = g // half_n
+            gz = g % half_n * 2
+            for core in range(2):
+                for zl in range(2):
+                    bi, ai = (gy, gz + zl) if core == 0 else (gz + zl, gy)
+                    dens = jnp.zeros((row_count, HD), F32)
+                    for r in range(count):
+                        first = r * group_rows + (core * 2 + zl) * row_count
+                        block = sums[last, pl.ds(first, row_count), :]
+                        part[core, bi, ai * count + r] = block[:, :HD].astype(BF16)
+                        dens = jnp.where(lane % 8 == r, block[:, HD:], dens)
+                    old = part[core, bi, tiles].astype(F32)
+                    part[core, bi, tiles] = jnp.where(lane // 8 == ai, dens, old).astype(BF16)
+            return carry
+
+        lax.fori_loop(0, groups, one_group, 0)
+        for d in far_first(n) + [0]:
+            j = (a + d) % n
+            send(
+                rcopy(
+                    part.at[1 - c, j],
+                    sibling_part[ch].at[j],
+                    p_send.at[3 * ch, d],
+                    p_recv.at[3 * ch, j],
+                    sib,
+                )
+            )
+
+    def sum_cores(ch):
+        part, core_sum = part_all[ch], core_sum_all[ch]
+        for d in far_first(n) + [0]:
+            j = (b + d) % n
+            rcopy(
+                part.at[1 - c, j],
+                sibling_part[ch].at[j],
+                p_send.at[3 * ch, d],
+                p_recv.at[3 * ch, j],
+                sib,
+            ).wait_recv()
+            core_sum[j] = (part[c, j].astype(F32) + sibling_part[ch][j].astype(F32)).astype(BF16)
+            if d:
+                send(
+                    rcopy(
+                        core_sum.at[j],
+                        b_parts[ch].at[b],
+                        p_send.at[3 * ch + 1, d],
+                        p_recv.at[3 * ch + 1, b],
+                        dev_b(j),
+                    )
+                )
+
+    pass_on(0)
+    await_sibling(0)
     loads[0].wait()
     loads[1].wait()
-    half_n = n // 2
-    group_rows = 4 * row_count
-
-    def one_slot(s):
-        group = slot_group[s]
-        gy = group // half_n
-        gz = group % half_n * 2
-        q = jnp.concatenate(
-            [qfull[0, gy, gz], qfull[0, gy, gz + 1], qfull[1, gz, gy], qfull[1, gz + 1, gy]],
-            axis=0,
-        )
-        q = jnp.concatenate([q[:, r * HD : (r + 1) * HD] for r in range(heads)], axis=0)
-        scores = lax.dot_general(
-            q, keys[s], (((1,), (1,)), ((), ())), preferred_element_type=F32
-        )
-        ok = iota(scores.shape, 1) < slot_limit[s]
-        weights = jnp.where(ok, jnp.exp(scores * scale), 0.0).astype(BF16)
-        extended = jnp.concatenate([values[s], jnp.ones((BLK, HD), BF16)], axis=1)
-        sums[s] = dot(weights, extended)
-
-    def slot_block(s, carry):
-        for i in range(4):
-            one_slot(s * 4 + i)
-        return carry
-
-    lax.fori_loop(0, slots // 4, slot_block, 0)
-
-    def link_slot(s, carry):
-        sums[s] = sums[s] + sums[slot_prev[s]]
-        return carry
-
-    lax.fori_loop(0, slots, link_slot, 0)
-
-    lane = iota((row_count, HD), 1)
-    tiles = n * heads
-    for core in range(2):
-        for j in range(n):
-            part[core, j, tiles] = jnp.zeros((row_count, HD), BF16)
-
-    def one_group(g, carry):
-        last = group_last[g]
-        gy = g // half_n
-        gz = g % half_n * 2
-        for core in range(2):
-            for zl in range(2):
-                bi, ai = (gy, gz + zl) if core == 0 else (gz + zl, gy)
-                dens = jnp.zeros((row_count, HD), F32)
-                for r in range(heads):
-                    first = r * group_rows + (core * 2 + zl) * row_count
-                    block = sums[last, pl.ds(first, row_count), :]
-                    part[core, bi, ai * heads + r] = block[:, :HD].astype(BF16)
-                    dens = jnp.where(lane % 8 == r, block[:, HD:], dens)
-                old = part[core, bi, tiles].astype(F32)
-                part[core, bi, tiles] = jnp.where(lane // 8 == ai, dens, old).astype(BF16)
-        return carry
-
-    lax.fori_loop(0, groups, one_group, 0)
-
-    p_send, p_recv = part_sems
-    for d in far_first(n) + [0]:
-        j = (a + d) % n
-        send(rcopy(part.at[1 - c, j], sibling_part.at[j], p_send.at[0, d], p_recv.at[0, j], sib))
-    for d in far_first(n) + [0]:
-        j = (b + d) % n
-        rcopy(
-            part.at[1 - c, j], sibling_part.at[j], p_send.at[0, d], p_recv.at[0, j], sib
-        ).wait_recv()
-        core_sum[j] = (part[c, j].astype(F32) + sibling_part[j].astype(F32)).astype(BF16)
-        if d:
-            send(rcopy(core_sum.at[j], b_parts.at[b], p_send.at[1, d], p_recv.at[1, b], dev_b(j)))
+    attend(0)
+    pass_on(1)
+    sum_cores(0)
+    await_sibling(1)
+    attend(1)
+    sum_cores(1)
 
     for j in range(1, 4):
         p = (group_place + j) % 4
@@ -400,65 +458,92 @@
     pick_t = jnp.transpose(pick).astype(BF16)
     spread = (iota((experts, cols), 0) == col_expert).astype(F32)
 
-    for d in near_first(n):
-        j = (b + d) % n
-        rcopy(core_sum.at[j], b_parts.at[j], p_send.at[1, d], p_recv.at[1, j], dev_b(j)).wait_recv()
-    dens = core_sum[b, tiles].astype(F32)
-    for e in range(1, n):
-        dens = dens + b_parts[(b + e) % n, tiles].astype(F32)
-    dens = dens.astype(BF16)
-    for d in far_first(n) + [0]:
-        j = (a + d) % n
-        chunk = pl.ds(j * heads, heads)
-        total = core_sum[b, chunk].astype(F32)
+    for ch, (first_head, last_head) in enumerate(spans):
+        count = last_head - first_head
+        core_sum, part_b, sum_b = core_sum_all[ch], b_parts[ch], b_sum[ch]
+        for d in near_first(n):
+            j = (b + d) % n
+            rcopy(
+                core_sum.at[j], part_b.at[j], p_send.at[3 * ch + 1, d], p_recv.at[3 * ch + 1, j], dev_b(j)
+            ).wait_recv()
+        dens = core_sum[b, n * count].astype(F32)
         for e in range(1, n):
-            total = total + b_parts[(b + e) % n, chunk].astype(F32)
-        b_sum[j, 0:heads] = total.astype(BF16)
-        b_sum[j, heads] = dens
-        if d:
-            send(rcopy(b_sum.at[j], a_parts.at[a], p_send.at[2, d], p_recv.at[2, a], dev_a(j)))
-    total = b_sum[a].astype(F32)
-    for d in near_first(n):
-        j = (a + d) % n
-        rcopy(b_sum.at[j], a_parts.at[j], p_send.at[2, d], p_recv.at[2, j], dev_a(j)).wait_recv()
-        total = total + a_parts[j].astype(F32)
+            dens = dens + part_b[(b + e) % n, n * count].astype(F32)
+        dens = dens.astype(BF16)
+        for d in far_first(n) + [0]:
+            j = (a + d) % n
+            chunk = pl.ds(j * count, count)
+            total = core_sum[b, chunk].astype(F32)
+            for e in range(1, n):
+                total = total + part_b[(b + e) % n, chunk].astype(F32)
+            sum_b[j, 0:count] = total.astype(BF16)
+            sum_b[j, count] = dens
+            if d:
+                send(
+                    rcopy(
+                        sum_b.at[j],
+                        a_parts[ch].at[a],
+                        p_send.at[3 * ch + 2, d],
+                        p_recv.at[3 * ch + 2, a],
+                        dev_a(j),
+                    )
+                )
+    nums = []
+    dens = []
+    for ch, (first_head, last_head) in enumerate(spans):
+        count = last_head - first_head
+        total = b_sum[ch][a].astype(F32)
+        for d in near_first(n):
+            j = (a + d) % n
+            rcopy(
+                b_sum[ch].at[j], a_parts[ch].at[j], p_send.at[3 * ch + 2, d], p_recv.at[3 * ch + 2, j], dev_a(j)
+            ).wait_recv()
+            total = total + a_parts[ch][j].astype(F32)
+        for r in range(count):
+            nums.append(total[r])
+            mine = jnp.where(lane == a * 8 + r, total[count], 0.0)
+            dens.append(jnp.sum(mine, axis=1, keepdims=True))
 
     attended = []
     for r in range(heads):
-        num = total[r] + tail_num[r * row_count : (r + 1) * row_count]
-        mine = jnp.sum(jnp.where(lane == a * 8 + r, total[heads], 0.0), axis=1, keepdims=True)
-        den = mine + tail_den[r * row_count : (r + 1) * row_count]
+        num = nums[r] + tail_num[r * row_count : (r + 1) * row_count]
+        den = dens[r] + tail_den[r * row_count : (r + 1) * row_count]
         attended.append((num / den).astype(BF16).astype(F32))
     residual = (stream_ref[...].reshape(row_count, width).astype(F32) + jnp.concatenate(attended, axis=1)).astype(BF16)
     resid[...] = residual
 
     x_ssem, x_rsem = x_sems
-    for d in range(1, kv_count):
+    spots = [(dx, d) for d in far_first(n) + [0] for dx in far_first(kv_count) + [0]]
+    for dx, d in spots[:-1]:
+        device = dev_xb((kv + dx) % kv_count, (b + d) % n)
         send(
             rcopy(
-                resid, resid_all.at[kv], x_ssem.at[0, d], x_rsem.at[0, kv], dev_x((kv + d) % kv_count)
+                resid,
+                mid_resid.at[b, kv],
+                x_ssem.at[0, dx * n + d],
+                x_rsem.at[0, kv * n + b],
+                device,
             )
         )
-    resid_all[kv] = residual
+    mid_resid[b, kv] = residual
     loads[2].wait()
     loads[5].wait()
-    for d in range(1, kv_count):
-        j = (kv + d) % kv_count
-        rcopy(resid, resid_all.at[j], x_ssem.at[0, d], x_rsem.at[0, j], dev_x(j)).wait_recv()
-    full = jnp.concatenate([resid_all[i].astype(F32) for i in range(kv_count)], axis=1)
-    mean_square = jnp.sum(full * full, axis=1, keepdims=True) / full.shape[1]
-    normed = (full * lax.rsqrt(mean_square + 1e-06) * gain[...]).astype(BF16)
+    for dx, d in reversed(spots[:-1]):
+        i, j = (kv + dx) % kv_count, (b + d) % n
+        rcopy(
+            resid, mid_resid.at[j, i], x_ssem.at[0, dx * n + d], x_rsem.at[0, i * n + j], dev_xb(i, j)
+        ).wait_recv()
+    full = jnp.concatenate(
+        [
+            jnp.concatenate([mid_resid[j, i] for j in range(n)], axis=0).astype(F32)
+            for i in range(kv_count)
+        ],
+        axis=1,
+    )
+    mean_square = jnp.sum(full * full, axis=1, keepdims=True) / model
+    mid = (full * lax.rsqrt(mean_square + 1e-06) * gain[...]).astype(BF16)
 
     r_send, r_recv = row_sems
-    normed_own[...] = normed
-    for d in far_first(n):
-        j = (b + d) % n
-        send(rcopy(normed_own, mid_rows.at[b], r_send.at[0, d], r_recv.at[0, b], dev_b(j)))
-    mid_rows[b] = normed
-    for d in near_first(n):
-        j = (b + d) % n
-        rcopy(normed_own, mid_rows.at[j], r_send.at[0, d], r_recv.at[0, j], dev_b(j)).wait_recv()
-    mid = jnp.concatenate([mid_rows[j] for j in range(n)], axis=0)
     mid_perm[...] = dot(pick_t, mid).astype(BF16).reshape(mid_perm.shape)
     for d in far_first(n):
         j = (a + d) % n
@@ -520,25 +605,29 @@
             expert_part.at[i], expert_sib.at[i], e_send.at[0, d], e_recv.at[0, i], sib
         ).wait_recv()
         both = own_out + expert_sib[i].astype(F32)
-        if d:
-            x_send[i] = both.astype(BF16)
-            send(rcopy(x_send.at[i], x_recv.at[kv], e_send.at[1, d], e_recv.at[1, kv], dev_x(i)))
-    mine = both
-    for d in range(1, kv_count):
-        j = (kv + d) % kv_count
-        rcopy(x_send.at[j], x_recv.at[j], e_send.at[1, d], e_recv.at[1, j], dev_x(j)).wait_recv()
-        mine = mine + x_recv[j].astype(F32)
-
-    back_a[...] = mine.astype(BF16).reshape(back_a.shape)
-    for d in far_first(n):
-        j = (a + d) % n
-        send(rcopy(back_a.at[j], back_mid.at[a], e_send.at[2, d], e_recv.at[2, a], dev_a(j)))
-    back_mid[a] = back_a[a]
-    for d in near_first(n):
-        j = (a + d) % n
-        rcopy(back_a.at[j], back_mid.at[j], e_send.at[2, d], e_recv.at[2, j], dev_a(j)).wait_recv()
-    returned = back_mid[...].reshape(cols, width)
-    weighted = dot(share_high, returned) + dot(share_low, returned)
+        x_send[i] = both.astype(BF16).reshape(x_send.shape[1:])
+        for da in far_first(n) + [0]:
+            j = (a + da) % n
+            if d or da:
+                send(
+                    rcopy(
+                        x_send.at[i, j],
+                        back_mid.at[kv, a],
+                        x_ssem.at[1, d * n + da],
+                        x_rsem.at[1, kv * n + a],
+                        dev_xa(i, j),
+                    )
+                )
+    back_mid[kv, a] = x_send[kv, a]
+
+    shares = [jnp.concatenate([part] * kv_count, axis=1) for part in (share_high, share_low)]
+    for dx, d in [(dx, d) for d in [0] + near_first(n) for dx in range(kv_count)][1:]:
+        i, j = (kv + dx) % kv_count, (a + d) % n
+        rcopy(
+            x_send.at[i, j], back_mid.at[i, j], x_ssem.at[1, dx * n + d], x_rsem.at[1, i * n + j], dev_xa(i, j)
+        ).wait_recv()
+    returned = back_mid[...].reshape(kv_count * cols, width)
+    weighted = dot(shares[0], returned) + dot(shares[1], returned)
     back_sum[...] = weighted.astype(BF16).reshape(back_sum.shape)
     for d in far_first(n):
         j = (b + d) % n
@@ -582,7 +671,8 @@
     units = gate_w.shape[2]
     cols = n * n * MOST
     block = n * MOST
-    tiles = n * heads + 1
+    spans = [(heads + 1) // 2, heads // 2]
+    per_span = lambda shape, dtype: [vmem(shape(count), dtype) for count in spans]
     dma = pltpu.SemaphoreType.DMA
     vmem = pltpu.VMEM
     sems = lambda stages: (dma((stages, max(n, 4))), dma((stages, max(n, 4))))
@@ -607,36 +697,33 @@
             vmem((1, model), F32),
             dma((6 + kv_count,)),
             vmem((rows, width), BF16),
-            vmem((2, n, n, rows, width), BF16),
+            per_span(lambda k: (rows, k * HD), BF16),
+            per_span(lambda k: (2, n, n, rows, k * HD), BF16),
             vmem((4, rows, 2 * HD), BF16),
             vmem((n, rows, routes.shape[2]), jnp.int32),
-            sems(5),
+            sems(8),
             pltpu.SMEM((slots,), jnp.int32),
             pltpu.SMEM((slots,), jnp.int32),
             pltpu.SMEM((slots,), jnp.int32),
             pltpu.SMEM((groups,), jnp.int32),
-            vmem((slots + 1, 4 * rows * heads, 2 * HD), F32),
-            vmem((2, n, tiles, rows, HD), BF16),
-            vmem((n, tiles, rows, HD), BF16),
-            vmem((n, tiles, rows, HD), BF16),
-            vmem((n, tiles, rows, HD), BF16),
-            vmem((n, heads + 1, rows, HD), BF16),
-            vmem((n, heads + 1, rows, HD), BF16),
-            sems(3),
+            per_span(lambda k: (slots + 1, 4 * rows * k, 2 * HD), F32),
+            per_span(lambda k: (2, n, n * k + 1, rows, HD), BF16),
+            per_span(lambda k: (n, n * k + 1, rows, HD), BF16),
+            per_span(lambda k: (n, n * k + 1, rows, HD), BF16),
+            per_span(lambda k: (n, n * k + 1, rows, HD), BF16),
+            per_span(lambda k: (n, k + 1, rows, HD), BF16),
+            per_span(lambda k: (n, k + 1, rows, HD), BF16),
+            sems(6),
             vmem((rows, width), BF16),
-            vmem((kv_count, rows, width), BF16),
-            sems(1),
-            vmem((rows, model), BF16),
-            vmem((n, rows, model), BF16),
+            vmem((n, kv_count, rows, width), BF16),
+            (dma((2, kv_count * n)), dma((2, kv_count * n))),
             vmem((n, block, model), BF16),
             vmem((2, n, block, model), BF16),
             sems(3),
             vmem((kv_count, cols, width), BF16),
             vmem((kv_count, cols, width), BF16),
-            vmem((kv_count, cols, width), BF16),
-            vmem((kv_count, cols, width), BF16),
-            vmem((n, block, width), BF16),
-            vmem((n, block, width), BF16),
+            vmem((kv_count, n, block, width), BF16),
+            vmem((kv_count, n, block, width), BF16),
             vmem((n, rows, width), BF16),
             vmem((n, rows, width), BF16),
             sems(4),

time: 103 us -> 95.6 us (0.928)
  Pallas kernels: 101 us -> 94.1 us
    pallas_call x1, Pallas kernels: 101 us -> 94.1 us  [local(): pl.pallas_call(functools.partial(kernel, n, kv_count, heads), out_shape=j...]
where the time goes in v3:
time: 95.6 us; the launch traced here: 95.4 us
  Pallas kernels  94.1 us (98%)
  local copies, waits for them, and re-layouts  1.31 us (1%)
    pallas_call x1, Pallas kernels, local(): pl.pallas_call(functools.partial(kernel, n, kv_count, heads), out_shape=j...  94.1 us

profile of v3, /device:TPU:1, one launch (start us, length us, event | category | flops | bytes accessed | tf_op | source)
XLA Modules:
  0.0 95.4 jit_solution(2638336490727902035)
XLA Ops:
  0.0 94.1 %layer.1 = bf16[2,4,640]{2,1,0:T(4,128)(2,1)} custom-call(bf16[2,4,640]{2,1,0:T(4,128)(2,1)} %stream_ref.1, bf16[2,4,640]{2,1,0:T(4,128)(2,1)} %query_ref.1, bf16[2,4,2,128]{3,2,1,0:T(2,128)(2,1)} %newkv_ref.1, bf16[1,16,128,128]{3,2,1,0:T(8,128)(2,1)} %keys_hbm.1, bf16[1,16,128,128]{3,2,1,0:T(8,128)(2,1)} %values_hbm.1, s32[32]{0:T(128)} %lengths_ref.1, ...), custom_call_target="tpu_custom_call" | custom-call | tf_op jit(solution)/shard_map/layer/pallas_call | solution.py:682
  94.1 1.3 %copy.16 = bf16[2,4,640]{2,1,0:T(4,128)(2,1)} copy(bf16[2,4,640]{2,1,0:T(4,128)(2,1)} %layer.1) | data formatting | bytes 20480

commit v4 on v3

--- a/solution.py
+++ b/solution.py
@@ -72,6 +72,7 @@
     down,
     gain,
     load_sem,
+    weight_sems,
     query,
     query_parts,
     q_all,
@@ -93,11 +94,10 @@
     resid,
     mid_resid,
     x_sems,
+    line_ready,
     mid_perm,
     rows,
     row_sems,
-    expert_part,
-    expert_sib,
     x_send,
     back_mid,
     back_sum,
@@ -121,6 +121,8 @@
     blocks = table_ref.shape[1]
     steps = parents_ref.shape[0] + 1
     top = routes_ref.shape[1]
+    units = gate.shape[0] // 2
+    w_send, w_recv = weight_sems
     model = kv_count * width
     cols = n * n * MOST
     block_rows = n * MOST
@@ -151,18 +153,16 @@
                 (keys_hbm.at[0], keys),
                 (values_hbm.at[0], values),
                 (router_hbm, router),
-                (gate_hbm.at[0], gate),
-                (up_hbm.at[0], up),
+                (gate_hbm.at[0], gate.at[0:units]),
+                (up_hbm.at[0], up.at[0:units]),
                 (gain_hbm, gain.at[0]),
             ]
             + [
-                (down_hbm.at[0, :, i * width : (i + 1) * width], down.at[i])
+                (down_hbm.at[0, :, i * width : (i + 1) * width], down.at[i, 0:units])
                 for i in range(kv_count)
             ]
         )
     ]
-    for load in loads:
-        load.start()
     query[...] = query_ref[...].reshape(query.shape)
     for (first, last), share_q, all_q in zip(spans, query_parts, q_all):
         share_q[...] = query[:, first * HD : last * HD]
@@ -172,15 +172,14 @@
 
     barrier = pltpu.get_barrier_semaphore()
     greeted = 0
-    line = far_first(n)
-    for dx in range(kv_count):
-        i = (kv + dx) % kv_count
-        devices = [dev_xa(i, (a + d) % n) for d in line] + [dev_xb(i, (b + d) % n) for d in line]
-        if dx:
-            devices.append(dev_xa(i, a))
-        for device in devices:
+    for d in far_first(n):
+        for device in (dev_a((a + d) % n), dev_b((b + d) % n)):
             pl.semaphore_signal(barrier, inc=1, device_id=device, device_id_type=MESH)
             greeted += 1
+    kv_peers = [{"kv": (kv + d) % kv_count} for d in range(1, kv_count)]
+    for device in kv_peers:
+        pl.semaphore_signal(barrier, inc=1, device_id=device, device_id_type=MESH)
+        greeted += 1
     for d in range(1, 4):
         pl.semaphore_signal(
             barrier,
@@ -209,6 +208,10 @@
                     dev_a((a + d) % n),
                 )
             )
+    for load in loads[:2]:
+        load.start()
+    for device in kv_peers:
+        pl.semaphore_signal(line_ready, inc=1, device_id=device, device_id_type=MESH)
     for d in range(1, 4):
         peer = group_first + (group_place + d) % 4
         send(
@@ -245,6 +248,9 @@
                 dev_b((b + d) % n),
             )
         )
+
+    for load in loads[2:]:
+        load.start()
 
     table = table_ref[...]
     place = iota((groups, blocks), 0) * blocks + iota((groups, blocks), 1) + 1
@@ -388,17 +394,6 @@
                         dev_b(j),
                     )
                 )
-
-    pass_on(0)
-    await_sibling(0)
-    loads[0].wait()
-    loads[1].wait()
-    attend(0)
-    pass_on(1)
-    sum_cores(0)
-    await_sibling(1)
-    attend(1)
-    sum_cores(1)
 
     for j in range(1, 4):
         p = (group_place + j) % 4
@@ -430,33 +425,31 @@
     tail_num = dot(tail_w, tail_kv[:, HD:])
     tail_den = jnp.sum(tail_w.astype(F32), axis=1, keepdims=True)
 
-    for d in near_first(n):
-        j = (b + d) % n
-        rcopy(
-            routes_b.at[j], routes_b.at[j], q_send.at[4, d], q_recv.at[4, j], dev_b(j)
-        ).wait_recv()
-    routed = jnp.concatenate([routes_b[j] for j in range(n)], axis=0)
-    col = iota((1, cols), 1)
-    col_chip = col // block_rows
-    col_source = col // MOST % n
-    col_place = col % MOST
-    col_expert = b * n + col_chip + c * ((col_chip - b) * (n - 1))
-    experts = n * n
-    source = iota((mids, 1), 0) // row_count
-    expert_lane = iota((1, experts), 1)
-    hit = jnp.zeros((mids, cols), F32)
-    chosen = jnp.zeros((mids, experts), F32)
-    for i in range(top):
-        hit = jnp.where(routed[:, i : i + 1] == col_expert, 1.0, hit)
-        chosen = jnp.where(routed[:, i : i + 1] == expert_lane, 1.0, chosen)
-    hit = jnp.where(source == col_source, hit, 0.0)
-    first_id = iota((mids, mids), 0)
-    second_id = iota((mids, mids), 1)
-    earlier = (first_id > second_id) & (first_id // row_count == second_id // row_count)
-    taken = dot(earlier.astype(F32).astype(BF16), hit.astype(BF16))
-    pick = jnp.where(taken == col_place.astype(F32), hit, 0.0)
-    pick_t = jnp.transpose(pick).astype(BF16)
-    spread = (iota((experts, cols), 0) == col_expert).astype(F32)
+    pass_on(0)
+    await_sibling(0)
+    loads[0].wait()
+    loads[1].wait()
+    attend(0)
+    pass_on(1)
+    sum_cores(0)
+    await_sibling(1)
+    attend(1)
+    sum_cores(1)
+
+    for load in loads[3:5] + loads[6:]:
+        load.wait()
+    halves = [(gate, 0), (up, 1), (down, 2)]
+    for weight, i in halves:
+        rows_of = (slice(None),) * (len(weight.shape) - 2)
+        send(
+            rcopy(
+                weight.at[rows_of + (pl.ds(0, units),)],
+                weight.at[rows_of + (pl.ds(units, units),)],
+                w_send.at[i],
+                w_recv.at[i],
+                sib,
+            )
+        )
 
     for ch, (first_head, last_head) in enumerate(spans):
         count = last_head - first_head
@@ -513,6 +506,7 @@
     resid[...] = residual
 
     x_ssem, x_rsem = x_sems
+    pl.semaphore_wait(line_ready, kv_count - 1)
     spots = [(dx, d) for d in far_first(n) + [0] for dx in far_first(kv_count) + [0]]
     for dx, d in spots[:-1]:
         device = dev_xb((kv + dx) % kv_count, (b + d) % n)
@@ -526,6 +520,34 @@
             )
         )
     mid_resid[b, kv] = residual
+    for d in near_first(n):
+        j = (b + d) % n
+        rcopy(
+            routes_b.at[j], routes_b.at[j], q_send.at[4, d], q_recv.at[4, j], dev_b(j)
+        ).wait_recv()
+    routed = jnp.concatenate([routes_b[j] for j in range(n)], axis=0)
+    col = iota((1, cols), 1)
+    col_chip = col // block_rows
+    col_source = col // MOST % n
+    col_place = col % MOST
+    col_expert = b * n + col_chip + c * ((col_chip - b) * (n - 1))
+    experts = n * n
+    source = iota((mids, 1), 0) // row_count
+    expert_lane = iota((1, experts), 1)
+    hit = jnp.zeros((mids, cols), F32)
+    chosen = jnp.zeros((mids, experts), F32)
+    for i in range(top):
+        hit = jnp.where(routed[:, i : i + 1] == col_expert, 1.0, hit)
+        chosen = jnp.where(routed[:, i : i + 1] == expert_lane, 1.0, chosen)
+    hit = jnp.where(source == col_source, hit, 0.0)
+    first_id = iota((mids, mids), 0)
+    second_id = iota((mids, mids), 1)
+    earlier = (first_id > second_id) & (first_id // row_count == second_id // row_count)
+    taken = dot(earlier.astype(F32).astype(BF16), hit.astype(BF16))
+    pick = jnp.where(taken == col_place.astype(F32), hit, 0.0)
+    pick_t = jnp.transpose(pick).astype(BF16)
+    spread = (iota((experts, cols), 0) == col_expert).astype(F32)
+
     loads[2].wait()
     loads[5].wait()
     for dx, d in reversed(spots[:-1]):
@@ -547,9 +569,8 @@
     mid_perm[...] = dot(pick_t, mid).astype(BF16).reshape(mid_perm.shape)
     for d in far_first(n):
         j = (a + d) % n
-        send(rcopy(mid_perm.at[j], rows.at[c, a], r_send.at[1, d], r_recv.at[1, a], dev_a(j)))
-    send(rcopy(mid_perm.at[a], rows.at[c, a], r_send.at[2, 0], r_recv.at[2, a], sib))
-    rows[c, a] = mid_perm[a]
+        send(rcopy(mid_perm.at[j], rows.at[a], r_send.at[d], r_recv.at[a], dev_a(j)))
+    rows[a] = mid_perm[a]
 
     logits = lax.dot_general(
         mid, router[...], (((1,), (1,)), ((), ())), preferred_element_type=F32
@@ -567,45 +588,22 @@
     share_high = share.astype(BF16)
     share_low = (share - share_high.astype(F32)).astype(BF16)
 
+    for weight, i in halves:
+        rows_of = (slice(None),) * (len(weight.shape) - 2)
+        half = weight.at[rows_of + (pl.ds(units, units),)]
+        rcopy(half, half, w_send.at[i], w_recv.at[i], sib).wait_recv()
     for d in near_first(n):
         j = (a + d) % n
-        rcopy(mid_perm.at[j], rows.at[c, j], r_send.at[1, d], r_recv.at[1, j], dev_a(j)).wait_recv()
-        send(rcopy(rows.at[c, j], rows.at[c, j], r_send.at[2, d], r_recv.at[2, j], sib))
-    loads[3].wait()
-    loads[4].wait()
-
-    def hidden(core):
-        x = rows[core].reshape(cols, model)
-        gated = lax.dot_general(
-            x, gate[...], (((1,), (1,)), ((), ())), preferred_element_type=F32
-        )
-        lifted = lax.dot_general(
-            x, up[...], (((1,), (1,)), ((), ())), preferred_element_type=F32
-        )
-        return (gated / (1.0 + jnp.exp(-gated)) * lifted).astype(BF16)
-
-    own_hidden = hidden(c)
-    for j in range(n):
-        rcopy(
-            rows.at[1 - c, j], rows.at[1 - c, j], r_send.at[2, j], r_recv.at[2, j], sib
-        ).wait_recv()
-    sib_hidden = hidden(1 - c)
-    for load in loads[6:]:
-        load.wait()
+        rcopy(mid_perm.at[j], rows.at[j], r_send.at[d], r_recv.at[j], dev_a(j)).wait_recv()
+    x = rows[...].reshape(cols, model)
+    turned = (((1,), (1,)), ((), ()))
+    gated = lax.dot_general(x, gate[...], turned, preferred_element_type=F32)
+    lifted = lax.dot_general(x, up[...], turned, preferred_element_type=F32)
+    hidden = (gated / (1.0 + jnp.exp(-gated)) * lifted).astype(BF16)
     e_send, e_recv = back_sems
-    slices = far_first(kv_count) + [0]
-    for d in slices:
+    for d in far_first(kv_count) + [0]:
         i = (kv + d) % kv_count
-        expert_part[i] = dot(sib_hidden, down[i]).astype(BF16)
-        send(rcopy(expert_part.at[i], expert_sib.at[i], e_send.at[0, d], e_recv.at[0, i], sib))
-    for d in slices:
-        i = (kv + d) % kv_count
-        own_out = dot(own_hidden, down[i])
-        rcopy(
-            expert_part.at[i], expert_sib.at[i], e_send.at[0, d], e_recv.at[0, i], sib
-        ).wait_recv()
-        both = own_out + expert_sib[i].astype(F32)
-        x_send[i] = both.astype(BF16).reshape(x_send.shape[1:])
+        x_send[i] = dot(hidden, down[i]).astype(BF16).reshape(x_send.shape[1:])
         for da in far_first(n) + [0]:
             j = (a + da) % n
             if d or da:
@@ -631,12 +629,12 @@
     back_sum[...] = weighted.astype(BF16).reshape(back_sum.shape)
     for d in far_first(n):
         j = (b + d) % n
-        send(rcopy(back_sum.at[j], back_rows.at[b], e_send.at[3, d], e_recv.at[3, b], dev_b(j)))
+        send(rcopy(back_sum.at[j], back_rows.at[b], e_send.at[d], e_recv.at[b], dev_b(j)))
     combined = resid[...].astype(F32) + back_sum[b].astype(F32)
     for d in near_first(n):
         j = (b + d) % n
         rcopy(
-            back_sum.at[j], back_rows.at[j], e_send.at[3, d], e_recv.at[3, j], dev_b(j)
+            back_sum.at[j], back_rows.at[j], e_send.at[d], e_recv.at[j], dev_b(j)
         ).wait_recv()
         combined = combined + back_rows[j].astype(F32)
     out_ref[...] = combined.astype(BF16).reshape(out_ref.shape)
@@ -691,11 +689,12 @@
             vmem((slots, BLK, HD), BF16),
             vmem((slots, BLK, HD), BF16),
             vmem((router.shape[1], model), BF16),
-            vmem((units, model), BF16),
-            vmem((units, model), BF16),
-            vmem((kv_count, units, width), BF16),
+            vmem((2 * units, model), BF16),
+            vmem((2 * units, model), BF16),
+            vmem((kv_count, 2 * units, width), BF16),
             vmem((1, model), F32),
             dma((6 + kv_count,)),
+            (dma((3,)), dma((3,))),
             vmem((rows, width), BF16),
             per_span(lambda k: (rows, k * HD), BF16),
             per_span(lambda k: (2, n, n, rows, k * HD), BF16),
@@ -717,16 +716,15 @@
             vmem((rows, width), BF16),
             vmem((n, kv_count, rows, width), BF16),
             (dma((2, kv_count * n)), dma((2, kv_count * n))),
+            pltpu.SemaphoreType.REGULAR,
             vmem((n, block, model), BF16),
-            vmem((2, n, block, model), BF16),
-            sems(3),
-            vmem((kv_count, cols, width), BF16),
-            vmem((kv_count, cols, width), BF16),
+            vmem((n, block, model), BF16),
+            (dma((n,)), dma((n,))),
             vmem((kv_count, n, block, width), BF16),
             vmem((kv_count, n, block, width), BF16),
             vmem((n, rows, width), BF16),
             vmem((n, rows, width), BF16),
-            sems(4),
+            (dma((n,)), dma((n,))),
         ],
         compiler_params=pltpu.CompilerParams(collective_id=0, has_side_effects=True),
         name="layer",

time: 95.6 us -> 91.2 us (0.954); the launches traced: 95.4 us -> 89.8 us
  Pallas kernels: 94.1 us -> 88.5 us
    pallas_call x1, Pallas kernels: 94.1 us -> 88.5 us  [local(): pl.pallas_call(functools.partial(kernel, n, kv_count, heads), out_shape=j...]
where the time goes in v4:
time: 91.2 us; the launch traced here: 89.8 us
  Pallas kernels  88.5 us (97%)
  local copies, waits for them, and re-layouts  1.31 us (1%)
    pallas_call x1, Pallas kernels, local(): pl.pallas_call(functools.partial(kernel, n, kv_count, heads), out_shape=j...  88.5 us

profile of v4, /device:TPU:1, one launch (start us, length us, event | category | flops | bytes accessed | tf_op | source)
XLA Modules:
  0.0 89.8 jit_solution(15757254038613940225)
XLA Ops:
  0.0 88.5 %layer.1 = bf16[2,4,640]{2,1,0:T(4,128)(2,1)} custom-call(bf16[2,4,640]{2,1,0:T(4,128)(2,1)} %stream_ref.1, bf16[2,4,640]{2,1,0:T(4,128)(2,1)} %query_ref.1, bf16[2,4,2,128]{3,2,1,0:T(2,128)(2,1)} %newkv_ref.1, bf16[1,16,128,128]{3,2,1,0:T(8,128)(2,1)} %keys_hbm.1, bf16[1,16,128,128]{3,2,1,0:T(8,128)(2,1)} %values_hbm.1, s32[32]{0:T(128)} %lengths_ref.1, ...), custom_call_target="tpu_custom_call" | custom-call | tf_op jit(solution)/shard_map/layer/pallas_call | solution.py:680
  88.5 1.3 %copy.16 = bf16[2,4,640]{2,1,0:T(4,128)(2,1)} copy(bf16[2,4,640]{2,1,0:T(4,128)(2,1)} %layer.1) | data formatting | bytes 20480

commit v5 on v4

--- a/solution.py
+++ b/solution.py
@@ -127,6 +127,8 @@
     cols = n * n * MOST
     block_rows = n * MOST
     mids = n * row_count
+    half_cols = cols // 2
+    half_rows = block_rows // 2
     scale = 1.0 / math.sqrt(HD)
 
     def dev_a(j):
@@ -525,10 +527,10 @@
         rcopy(
             routes_b.at[j], routes_b.at[j], q_send.at[4, d], q_recv.at[4, j], dev_b(j)
         ).wait_recv()
-    routed = jnp.concatenate([routes_b[j] for j in range(n)], axis=0)
+    routed = jnp.concatenate([routes_b[(b + p) % n] for p in range(n)], axis=0)
     col = iota((1, cols), 1)
-    col_chip = col // block_rows
-    col_source = col // MOST % n
+    col_chip = col % half_cols // half_rows
+    col_source = col // half_cols * half_n + col // MOST % half_n
     col_place = col % MOST
     col_expert = b * n + col_chip + c * ((col_chip - b) * (n - 1))
     experts = n * n
@@ -557,7 +559,7 @@
         ).wait_recv()
     full = jnp.concatenate(
         [
-            jnp.concatenate([mid_resid[j, i] for j in range(n)], axis=0).astype(F32)
+            jnp.concatenate([mid_resid[(b + p) % n, i] for p in range(n)], axis=0).astype(F32)
             for i in range(kv_count)
         ],
         axis=1,
@@ -566,11 +568,15 @@
     mid = (full * lax.rsqrt(mean_square + 1e-06) * gain[...]).astype(BF16)
 
     r_send, r_recv = row_sems
-    mid_perm[...] = dot(pick_t, mid).astype(BF16).reshape(mid_perm.shape)
-    for d in far_first(n):
-        j = (a + d) % n
-        send(rcopy(mid_perm.at[j], rows.at[a], r_send.at[d], r_recv.at[a], dev_a(j)))
-    rows[a] = mid_perm[a]
+    for u in (1, 0):
+        picked = dot(pick_t[u * half_cols : (u + 1) * half_cols], mid)
+        mid_perm[u] = picked.astype(BF16).reshape(mid_perm.shape[1:])
+        for d in far_first(n):
+            j = (a + d) % n
+            send(
+                rcopy(mid_perm.at[u, j], rows.at[u, a], r_send.at[u, d], r_recv.at[u, a], dev_a(j))
+            )
+        rows[u, a] = mid_perm[u, a]
 
     logits = lax.dot_general(
         mid, router[...], (((1,), (1,)), ((), ())), preferred_element_type=F32
@@ -592,49 +598,67 @@
         rows_of = (slice(None),) * (len(weight.shape) - 2)
         half = weight.at[rows_of + (pl.ds(units, units),)]
         rcopy(half, half, w_send.at[i], w_recv.at[i], sib).wait_recv()
-    for d in near_first(n):
-        j = (a + d) % n
-        rcopy(mid_perm.at[j], rows.at[j], r_send.at[d], r_recv.at[j], dev_a(j)).wait_recv()
-    x = rows[...].reshape(cols, model)
     turned = (((1,), (1,)), ((), ()))
-    gated = lax.dot_general(x, gate[...], turned, preferred_element_type=F32)
-    lifted = lax.dot_general(x, up[...], turned, preferred_element_type=F32)
-    hidden = (gated / (1.0 + jnp.exp(-gated)) * lifted).astype(BF16)
+    for u in (1, 0):
+        for d in near_first(n):
+            j = (a + d) % n
+            rcopy(
+                mid_perm.at[u, j], rows.at[u, j], r_send.at[u, d], r_recv.at[u, j], dev_a(j)
+            ).wait_recv()
+        x = rows[u].reshape(half_cols, model)
+        gated = lax.dot_general(x, gate[...], turned, preferred_element_type=F32)
+        lifted = lax.dot_general(x, up[...], turned, preferred_element_type=F32)
+        hidden = (gated / (1.0 + jnp.exp(-gated)) * lifted).astype(BF16)
+        for d in far_first(kv_count) + [0]:
+            i = (kv + d) % kv_count
+            x_send[u, i] = dot(hidden, down[i]).astype(BF16).reshape(x_send.shape[2:])
+            for da in far_first(n) + [0]:
+                j = (a + da) % n
+                if d or da:
+                    send(
+                        rcopy(
+                            x_send.at[u, i, j],
+                            back_mid.at[u, kv, a],
+                            x_ssem.at[1 + u, d * n + da],
+                            x_rsem.at[1 + u, kv * n + a],
+                            dev_xa(i, j),
+                        )
+                    )
+        back_mid[u, kv, a] = x_send[u, kv, a]
+
     e_send, e_recv = back_sems
-    for d in far_first(kv_count) + [0]:
-        i = (kv + d) % kv_count
-        x_send[i] = dot(hidden, down[i]).astype(BF16).reshape(x_send.shape[1:])
-        for da in far_first(n) + [0]:
-            j = (a + da) % n
-            if d or da:
+    half_mids = mids // 2
+    for u in (1, 0):
+        own_rows = slice(u * half_mids, (u + 1) * half_mids)
+        own_cols = slice(u * half_cols, (u + 1) * half_cols)
+        shares = [
+            jnp.concatenate([part[own_rows, own_cols]] * kv_count, axis=1)
+            for part in (share_high, share_low)
+        ]
+        for dx, d in [(dx, d) for d in [0] + near_first(n) for dx in range(kv_count)][1:]:
+            i, j = (kv + dx) % kv_count, (a + d) % n
+            rcopy(
+                x_send.at[u, i, j],
+                back_mid.at[u, i, j],
+                x_ssem.at[1 + u, dx * n + d],
+                x_rsem.at[1 + u, i * n + j],
+                dev_xa(i, j),
+            ).wait_recv()
+        returned = back_mid[u].reshape(kv_count * half_cols, width)
+        weighted = dot(shares[0], returned) + dot(shares[1], returned)
+        back_sum[u * half_n : (u + 1) * half_n] = weighted.astype(BF16).reshape((half_n,) + back_sum.shape[1:])
+        for p in far_first(n):
+            if p // half_n == u:
                 send(
                     rcopy(
-                        x_send.at[i, j],
-                        back_mid.at[kv, a],
-                        x_ssem.at[1, d * n + da],
-                        x_rsem.at[1, kv * n + a],
-                        dev_xa(i, j),
+                        back_sum.at[p], back_rows.at[b], e_send.at[p], e_recv.at[b], dev_b((b + p) % n)
                     )
                 )
-    back_mid[kv, a] = x_send[kv, a]
-
-    shares = [jnp.concatenate([part] * kv_count, axis=1) for part in (share_high, share_low)]
-    for dx, d in [(dx, d) for d in [0] + near_first(n) for dx in range(kv_count)][1:]:
-        i, j = (kv + dx) % kv_count, (a + d) % n
-        rcopy(
-            x_send.at[i, j], back_mid.at[i, j], x_ssem.at[1, dx * n + d], x_rsem.at[1, i * n + j], dev_xa(i, j)
-        ).wait_recv()
-    returned = back_mid[...].reshape(kv_count * cols, width)
-    weighted = dot(shares[0], returned) + dot(shares[1], returned)
-    back_sum[...] = weighted.astype(BF16).reshape(back_sum.shape)
-    for d in far_first(n):
-        j = (b + d) % n
-        send(rcopy(back_sum.at[j], back_rows.at[b], e_send.at[d], e_recv.at[b], dev_b(j)))
-    combined = resid[...].astype(F32) + back_sum[b].astype(F32)
+    combined = resid[...].astype(F32) + back_sum[0].astype(F32)
     for d in near_first(n):
         j = (b + d) % n
         rcopy(
-            back_sum.at[j], back_rows.at[j], e_send.at[d], e_recv.at[j], dev_b(j)
+            back_sum.at[d], back_rows.at[j], e_send.at[d], e_recv.at[j], dev_b(j)
         ).wait_recv()
         combined = combined + back_rows[j].astype(F32)
     out_ref[...] = combined.astype(BF16).reshape(out_ref.shape)
@@ -715,13 +739,13 @@
             sems(6),
             vmem((rows, width), BF16),
             vmem((n, kv_count, rows, width), BF16),
-            (dma((2, kv_count * n)), dma((2, kv_count * n))),
+            (dma((3, kv_count * n)), dma((3, kv_count * n))),
             pltpu.SemaphoreType.REGULAR,
-            vmem((n, block, model), BF16),
-            vmem((n, block, model), BF16),
-            (dma((n,)), dma((n,))),
-            vmem((kv_count, n, block, width), BF16),
-            vmem((kv_count, n, block, width), BF16),
+            vmem((2, n, block // 2, model), BF16),
+            vmem((2, n, block // 2, model), BF16),
+            (dma((2, n)), dma((2, n))),
+            vmem((2, kv_count, n, block // 2, width), BF16),
+            vmem((2, kv_count, n, block // 2, width), BF16),
             vmem((n, rows, width), BF16),
             vmem((n, rows, width), BF16),
             (dma((n,)), dma((n,))),

time: 91.2 us -> 89 us (0.976)
  Pallas kernels: 88.5 us -> 86 us
    pallas_call x1, Pallas kernels: 88.5 us -> 86 us  [local(): pl.pallas_call(functools.partial(kernel, n, kv_count, heads), out_shape=j...]
where the time goes in v5:
time: 89 us; the launch traced here: 87.3 us
  Pallas kernels  86 us (97%)
  local copies, waits for them, and re-layouts  1.31 us (1%)
    pallas_call x1, Pallas kernels, local(): pl.pallas_call(functools.partial(kernel, n, kv_count, heads), out_shape=j...  86 us

profile of v5, /device:TPU:1, one launch (start us, length us, event | category | flops | bytes accessed | tf_op | source)
XLA Modules:
  0.0 87.3 jit_solution(3675436468918099150)
XLA Ops:
  0.0 86.0 %layer.1 = bf16[2,4,640]{2,1,0:T(4,128)(2,1)} custom-call(bf16[2,4,640]{2,1,0:T(4,128)(2,1)} %stream_ref.1, bf16[2,4,640]{2,1,0:T(4,128)(2,1)} %query_ref.1, bf16[2,4,2,128]{3,2,1,0:T(2,128)(2,1)} %newkv_ref.1, bf16[1,16,128,128]{3,2,1,0:T(8,128)(2,1)} %keys_hbm.1, bf16[1,16,128,128]{3,2,1,0:T(8,128)(2,1)} %values_hbm.1, s32[32]{0:T(128)} %lengths_ref.1, ...), custom_call_target="tpu_custom_call" | custom-call | tf_op jit(solution)/shard_map/layer/pallas_call | solution.py:704
  86.0 1.3 %copy.16 = bf16[2,4,640]{2,1,0:T(4,128)(2,1)} copy(bf16[2,4,640]{2,1,0:T(4,128)(2,1)} %layer.1) | data formatting | bytes 20480

commit v6 on v5

--- a/solution.py
+++ b/solution.py
@@ -233,7 +233,7 @@
                 query_parts[ch], q_all[ch].at[c, b, j], q_send.at[7 * ch, d], q_recv.at[7 * ch, j], dev_a(j)
             ).wait_recv()
         block = q_all[ch].at[c, b]
-        for d in far_first(n):
+        for d in near_first(n):
             send(
                 rcopy(
                     block, block, q_send.at[1 + 4 * ch, d], q_recv.at[1 + 4 * ch, b], dev_b((b + d) % n)
@@ -376,7 +376,7 @@
 
     def sum_cores(ch):
         part, core_sum = part_all[ch], core_sum_all[ch]
-        for d in far_first(n) + [0]:
+        for d in near_first(n) + [0]:
             j = (b + d) % n
             rcopy(
                 part.at[1 - c, j],

time: 89 us -> 91 us (1.022)
  the two profiles are of different devices: /device:TPU:1 before, /device:TPU:8 now
where the time goes in v6:
time: 91 us; the launch traced here: 90.7 us
  Pallas kernels  89.4 us (98%)
  local copies, waits for them, and re-layouts  1.31 us (1%)
    pallas_call x1, Pallas kernels, local(): pl.pallas_call(functools.partial(kernel, n, kv_count, heads), out_shape=j...  89.4 us

profile of v6, /device:TPU:8, one launch (start us, length us, event | category | flops | bytes accessed | tf_op | source)
XLA Modules:
  0.0 90.7 jit_solution(851823986140627057)
XLA Ops:
  0.0 89.4 %layer.1 = bf16[2,4,640]{2,1,0:T(4,128)(2,1)} custom-call(bf16[2,4,640]{2,1,0:T(4,128)(2,1)} %stream_ref.1, bf16[2,4,640]{2,1,0:T(4,128)(2,1)} %query_ref.1, bf16[2,4,2,128]{3,2,1,0:T(2,128)(2,1)} %newkv_ref.1, bf16[1,16,128,128]{3,2,1,0:T(8,128)(2,1)} %keys_hbm.1, bf16[1,16,128,128]{3,2,1,0:T(8,128)(2,1)} %values_hbm.1, s32[32]{0:T(128)} %lengths_ref.1, ...), custom_call_target="tpu_custom_call" | custom-call | tf_op jit(solution)/shard_map/layer/pallas_call | solution.py:704
  89.4 1.3 %copy.16 = bf16[2,4,640]{2,1,0:T(4,128)(2,1)} copy(bf16[2,4,640]{2,1,0:T(4,128)(2,1)} %layer.1) | data formatting | bytes 20480
